TPU v7x, 256 devices: a whole 4x4x8 slice. The times are simulated.
256 devices in a mesh: vox: 64 (over y, x, z_lo), sen: 4 (over z_hi, core).
Axes of the slice: x: 4, y: 4, z: 8 (z_hi: 2, z_lo: 4; z = z_hi * 4 + z_lo), core: 2. Of those that a mesh axis runs over, the one named last changes fastest.
Arguments:
- image: float32 [64, 2, 512], P('vox'), may hold values from -6 to 6
- weights: bfloat16 [64, 4, 5, 1024, 1024], P('vox', 'sen'), may hold values from -0.0625 to 0.0625
- block_ids: int32 [64, 4, 5], P('vox', 'sen'), may hold values from 0 to 15
- offsets: int32 [64, 4, 5], P('vox', 'sen'), may hold values from 0 to 1984
- counts: int32 [64, 4], P('vox', 'sen'), may hold values from 1 to 5, as said below
- measured: bfloat16 [4, 256, 2048], P('sen', 'vox'), may hold values from -6 to 6
Outputs:
- image_next: float32 [64, 2, 512], P('vox')
- residual: float32 [4, 256, 2048], P('sen', 'vox')
Inputs may be any that keep to these rules, and one draw needn't show every extreme that they name: `counts`: some slab and group has all 5 slots live in every draw.
All inputs are finite; a program needn't handle non-finite values.
Results may differ from a plain program's by a relative error of at most 0.0025.
Values may be sent and summed in bfloat16 or wider, within the bound.
No kernel may reach another device: no remote copies, remote signals or barrier semaphores. Data moves between devices by JAX's collectives and lax.ppermute only.
A program may use at most 64 MiB of HBM per device.

v0:
```python
import jax
import jax.numpy as jnp
from jax import lax
from jax.sharding import PartitionSpec as P

SENSORS = 1024
SAMPLES = 2048
SB = 16
WIN = 64
K_MAX = 5


TAPS = ((-2, 1.0 / 12.0), (-1, -8.0 / 12.0), (1, 8.0 / 12.0), (2, -1.0 / 12.0))
STEP_SIZE = 0.25
TV_WEIGHT = 0.3
TV_EPS = 0.01


def extended(array, sides, width):
    for axis, dim in sides:
        count, length = (lax.axis_size(axis), array.shape[dim])
        up = [(i, (i + 1) % count) for i in range(count - 1)]
        down = [(j, i) for i, j in up]
        last = lax.slice_in_dim(array, length - width, length, axis=dim)
        initial = lax.slice_in_dim(array, 0, width, axis=dim)
        before = lax.ppermute(last, axis, up)
        after = lax.ppermute(initial, axis, down)
        array = jnp.concatenate([before, array, after], axis=dim)
    return array


def derivative(signal):
    length_t = signal.shape[-1]
    padded = jnp.pad(signal, [(0, 0)] * (signal.ndim - 1) + [(2, 2)])
    summed = jnp.zeros_like(signal)
    for shift_by, coefficient in TAPS:
        summed = summed + coefficient * padded[..., 2 + shift_by : 2 + shift_by + length_t]
    return summed


def forward_step(volume, axis_dim):
    length_a = volume.shape[axis_dim]
    ahead = jnp.concatenate(
        [
            lax.slice_in_dim(volume, 1, length_a, axis=axis_dim),
            lax.slice_in_dim(volume, length_a - 1, length_a, axis=axis_dim),
        ],
        axis=axis_dim,
    )
    return ahead - volume


def backward_shift(field, axis_dim):
    length_a = field.shape[axis_dim]
    zero_row = jnp.zeros_like(lax.slice_in_dim(field, 0, 1, axis=axis_dim))
    return jnp.concatenate(
        [zero_row, lax.slice_in_dim(field, 0, length_a - 1, axis=axis_dim)], axis=axis_dim
    )


def place_window(partial_value, piece, block_index, start):
    corner = (block_index * SB, start)
    current = lax.dynamic_slice(partial_value, corner, (SB, WIN))
    return lax.dynamic_update_slice(partial_value, current + piece, corner)


def slab_tv(image):
    planes_ext = extended(image, (("vox", 0),), 1)
    slab_planes = image.shape[0]
    is_first = lax.axis_index("vox") == 0
    is_last = lax.axis_index("vox") == lax.axis_size("vox") - 1
    plane_index = jnp.arange(slab_planes + 1)[:, None, None]
    lower = planes_ext[:-1]
    step_z = planes_ext[1:] - planes_ext[:-1]
    step_z = jnp.where(is_last & (plane_index == slab_planes), 0.0, step_z)
    step_y = forward_step(lower, 1)
    step_x = forward_step(lower, 2)
    magnitude = jnp.sqrt(step_z * step_z + step_y * step_y + step_x * step_x + TV_EPS)
    unit_z = jnp.where(is_first & (plane_index == 0), 0.0, step_z / magnitude)
    unit_y = step_y / magnitude
    unit_x = step_x / magnitude
    result = unit_z[:-1] - unit_z[1:]
    result = result + (backward_shift(unit_y, 1) - unit_y)[1:]
    result = result + (backward_shift(unit_x, 2) - unit_x)[1:]
    return result


def on_device(image, weights, block_ids, offsets, counts, measured):
    voxels = image.astype(jnp.bfloat16).reshape(-1)
    blocks = weights[0, 0]
    block_index = block_ids[0, 0]
    starts = offsets[0, 0]
    live_count = counts[0, 0]
    group_sens = SENSORS // lax.axis_size("sen")
    live = (jnp.arange(K_MAX) < live_count).astype(jnp.float32)
    pieces = (
        jnp.einsum("v,kvc->kc", voxels, blocks, preferred_element_type=jnp.float32) * live[:, None]
    )

    def cut_window(source, block_number, start):
        corner = (block_number * SB, start)
        return lax.dynamic_slice(source, corner, (SB, WIN)).reshape(SB * WIN)

    zero_partial = jnp.zeros((group_sens, SAMPLES), jnp.float32)

    def add_masked(slot, partial_value):
        return place_window(
            partial_value, pieces[slot].reshape(SB, WIN), block_index[slot], starts[slot]
        )

    partial_value = lax.fori_loop(0, K_MAX, add_masked, zero_partial)
    whole_measured = lax.all_gather(measured, "vox", axis=1, tiled=True)
    summed = lax.psum(partial_value[None], "vox")
    residual_all = derivative(summed) - whole_measured.astype(jnp.float32)
    adjoint_all = (-derivative(residual_all)).astype(jnp.bfloat16)[0]
    own_rows = measured.shape[1]
    residual = lax.dynamic_slice_in_dim(residual_all, lax.axis_index("vox") * own_rows, own_rows, 1)
    windows = jax.vmap(lambda number, start: cut_window(adjoint_all, number, start))(
        block_index, starts
    )
    windows = windows * live.astype(jnp.bfloat16)[:, None]
    grad_local = jnp.einsum("kc,kvc->v", windows, blocks, preferred_element_type=jnp.float32)
    backprojected = lax.psum(grad_local, "sen").reshape(image.shape)
    image_next = image - STEP_SIZE * (backprojected + TV_WEIGHT * slab_tv(image))
    return (image_next, residual)


def solution(mesh):
    placed = (
        P("vox", None, None),
        P("vox", "sen", None, None, None),
        P("vox", "sen", None),
        P("vox", "sen", None),
        P("vox", "sen"),
        P("sen", "vox", None),
    )
    return jax.shard_map(
        on_device,
        mesh=mesh,
        in_specs=placed,
        out_specs=(P("vox", None, None), P("sen", "vox", None)),
        check_vma=False,
    )
```

profile of v0, /device:TPU:1, one launch (start us, length us, event | category | flops | bytes accessed | tf_op | source)
XLA Modules:
  0.0 1129.4 jit_solution(18124372229311792243)
XLA Ops:
  7.2 4.4 collective-permute-start.1
  11.6 1.4 copy.10
  13.7 0.8 constant_dynamic-update-slice_fusion
  14.5 5.5 fusion.2
  19.9 0.1 bitcast_multiply_fusion
  20.0 0.2 broadcast_in_dim.30
  20.3 0.3 copy-done.2
  20.6 21.9 %while.14 = (s32[]{:T(128)}, f32[256,2048]{1,0:T(8,128)S(1)}, s32[5]{0:T(128)S(1)}, s32[5]{0:T(128)S(1)}, f32[5,1024]{1,0:T(8,128)S(1)}, /*index=5*/s32[]{:T(128)}, s32[1]{0:T(128)}, s32[]{:T(128)}, s32[]{:T(128)}, s32[]{:T(128)}) while((s32[]{:T(128)}, f32[256,2048]{1,0:T(8,128)S(1)}, s32[5]{0:T(128)S(1)}, s32[5]{0:T(128)S(1)}, ...), condition=%wide.region_1.0_spmd, body=%wide.region_0.0_spmd.sunk | while | flops 1033 | bytes 37093 | solution.py:111
  20.6 0.1 squeeze.43
  20.7 0.6 dynamic_slice.41
  21.8 0.6 dynamic_slice.42
  24.0 0.1 dynamic-slice_add_fusion.2
  24.1 0.9 dynamic_update_slice.8
  25.1 0.1 squeeze.43
  25.2 0.6 dynamic_slice.41
  26.3 0.6 dynamic_slice.42
  28.5 0.1 dynamic-slice_add_fusion.2
  28.6 0.8 dynamic_update_slice.8
  29.4 0.1 squeeze.43
  29.4 0.6 dynamic_slice.41
  30.6 0.6 dynamic_slice.42
  32.8 0.1 dynamic-slice_add_fusion.2
  32.8 0.9 dynamic_update_slice.8
  33.9 0.6 dynamic_slice.41
  35.0 0.6 dynamic_slice.42
  37.2 0.1 dynamic-slice_add_fusion.2
  37.3 0.8 dynamic_update_slice.8
  38.2 0.6 dynamic_slice.41
  39.3 0.6 dynamic_slice.42
  41.5 0.1 dynamic-slice_add_fusion.2
  41.6 0.9 dynamic_update_slice.8
  42.5 1.3 copy-done
  43.9 1.3 collective-permute-start
  45.2 0.1 slice.87
  45.3 0.1 slice.86
  45.4 3.4 collective-permute-done
  48.8 0.1 broadcast_select_fusion
  48.9 0.1 fusion.14
  49.0 273.1 %all-gather.2.cloned.1.call-done = bf16[1,256,2048]{2,0,1:T(2,128)(2,1)} async-done(((bf16[1,4,2048]{2,0,1:T(2,128)(2,1)}), bf16[1,256,2048]{2,0,1:T(2,128)(2,1)}) %all-gather.2.cloned.1.call-update) | async-done | bytes 1048592 | tf_op jit(solution)/shard_map/all_gather | solution.py:112
  322.1 719.4 %all-reduce.6.cloned.1.call-done = f32[1,256,2048]{2,1,0:T(8,128)} async-done(((f32[1,256,2048]{2,1,0:T(8,128)}), f32[1,256,2048]{2,1,0:T(8,128)}) %all-reduce.6.cloned.1.call-update) | async-done | bytes 2097168 | tf_op jit(solution)/shard_map/psum | solution.py:113
  1041.5 6.5 convert_subtract_fusion
  1048.0 2.2 fusion.6
  1050.2 10.0 while.15
  1050.2 0.1 constant_dynamic-slice_fusion.3
  1050.3 0.5 fusion.19
  1050.8 1.4 bitcast_dynamic-update-slice_fusion.2
  1052.2 0.1 constant_dynamic-slice_fusion.3
  1052.3 0.5 fusion.19
  1052.8 1.4 bitcast_dynamic-update-slice_fusion.2
  1054.2 0.1 constant_dynamic-slice_fusion.3
  1054.3 0.5 fusion.19
  1054.8 1.4 bitcast_dynamic-update-slice_fusion.2
  1056.2 0.1 constant_dynamic-slice_fusion.3
  1056.3 0.5 fusion.19
  1056.8 1.4 bitcast_dynamic-update-slice_fusion.2
  1058.2 0.1 constant_dynamic-slice_fusion.3
  1058.3 0.5 fusion.19
  1058.8 1.4 bitcast_dynamic-update-slice_fusion.2
  1060.2 0.1 reshape.87
  1060.3 0.1 multiply_bitcast_fusion
  1060.4 6.8 fusion
  1067.2 54.1 %psum.15 = f32[1,2,512]{2,1,0:T(2,128)S(1)} all-reduce(f32[1,2,512]{2,1,0:T(2,128)S(1)} %reshape.88), channel_id=1, replica_groups=mesh['vox'=64,'sen'=4] {'sen'}, use_global_device_ids=true, to_apply=%region_3.4 | all-reduce | flops 1024 | bytes 8192 | tf_op jit(solution)/shard_map/psum | solution.py:123
  1121.3 0.6 constant_dynamic-slice_fusion.1
  1121.9 0.7 multiply_subtract_fusion
  (28 shorter events, 0.4 us)
Async XLA Ops:
  7.2 314.9 %all-gather.2.cloned.1.call-start = ((), (), s32[]{:S(2)}) async-start(), calls=%async_computation.1 | async-start | bytes 2129920 | tf_op jit(solution)/shard_map/all_gather | solution.py:112
  7.2 6.5 collective-permute-start.1
  13.0 1028.5 %all-reduce.6.cloned.1.call-start = ((), (), s32[]{:S(2)}) async-start(), calls=%async_computation | async-start | bytes 4194304 | tf_op jit(solution)/shard_map/psum | solution.py:113
  19.9 0.7 copy-start.2
  19.9 0.7 copy-start.3
  20.0 23.8 %copy-start.1 = (f32[1,2,512]{2,1,0:T(2,128)S(1)}, f32[1,2,512]{2,1,0:T(2,128)}, u32[]{:S(2)}) copy-start(f32[1,2,512]{2,1,0:T(2,128)} %param.8) | copy-start | bytes 12292
  42.5 1.3 copy-start
  43.9 4.9 collective-permute-start
Sparse Core Ops, SparseCore 0:
  13.1 308.9 all-gather.1
  324.7 716.7 all-reduce.5
where the time goes:
time: 1130 us
  waiting for transfers between devices  996 us (88%)
  blocking collectives  54.1 us (5%)
  local copies, waits for them, and re-layouts  24.4 us (2%)
  between operations  14.8 us (1%)
  matrix products  12.3 us (1%)
    psum x1, waiting for transfers between devices, on_device(): summed = lax.psum(partial_value[None], 'vox')  719 us
    all_gather x1, waiting for transfers between devices, on_device(): whole_measured = lax.all_gather(measured, 'vox', axis=1, tiled=True)  273 us
    psum x1, blocking collectives, on_device(): backprojected = lax.psum(grad_local, 'sen').reshape(image.shape)  54.1 us
  transfers between devices with their start and end apart: 4, of which 3 were waited for; matrix products, arithmetic and copies ran while one was open for 2% of the time, Pallas kernels for 0%

commit v1 on v0

v1 whole, which is shorter than its diff:
```python
import functools

import jax
import jax.numpy as jnp
from jax import lax
from jax.experimental import pallas as pl
from jax.experimental.pallas import tpu as pltpu
from jax.sharding import Mesh
from jax.sharding import PartitionSpec as P

SB = 16
WIN = 64
K_MAX = 5
VOXELS = 1024
CELLS = SB * WIN
LANES = 128
ROWS = 16
OWNERS = 64
CHUNKS = 2
STEP_SIZE = 0.25
TV_WEIGHT = 0.3
TV_EPS = 0.01
NOWHERE = 255.0
MIB = 1 << 20

VOX = ("y", "x", "z_lo")
SEN = ("z_hi", "core")


def lane_iota(shape):
    return lax.broadcasted_iota(jnp.int32, shape, len(shape) - 1)


def forward_kernel(ids, starts, counts, image, weights, measured, sent, spread, held, tiles, sems):
    depth = VOXELS // CHUNKS
    copies = {}
    for k in range(K_MAX):
        for c in range(CHUNKS):
            span = pl.ds(c * depth, depth)
            copies[k, c] = pltpu.make_async_copy(
                weights.at[0, 0, k, span], held.at[k, span], sems.at[k * CHUNKS + c]
            )
            copies[k, c].start()

    own = measured[0].astype(jnp.float32)
    for r in range(4):
        for h in range(16):
            spread[r * 16 + h : r * 16 + h + 1, :] = own[r : r + 1, h * LANES : (h + 1) * LANES]

    voxels = jnp.concatenate([image[0, 0:1, :], image[0, 1:2, :]], axis=1).astype(jnp.bfloat16)
    lane = lane_iota((8, LANES))
    row16 = lax.broadcasted_iota(jnp.int32, (ROWS, LANES), 0)
    lane16 = lane_iota((ROWS, LANES))
    base = jnp.full((ROWS, LANES), NOWHERE, jnp.float32)
    code_tile = jnp.full((ROWS, LANES), NOWHERE, jnp.float32)
    block_tile = jnp.full((ROWS, LANES), -1, jnp.int32)
    live = counts[0, 0]
    for k in range(K_MAX):
        start = starts[0, 0, k]
        coarse = start // WIN
        low = start - coarse * WIN
        code = (coarse & 1) * 16 + (coarse >> 1)
        block = jnp.where(k < live, ids[0, 0, k], -1)
        here = row16 == 10 + k
        base = jnp.where(here & (lane16 >= WIN), low.astype(jnp.float32), base)
        code_tile = jnp.where(here & (lane16 < WIN), code.astype(jnp.float32), code_tile)
        block_tile = jnp.where(here & (lane16 < WIN), block, block_tile)

    for k in range(K_MAX):
        piece = jnp.zeros((1, CELLS), jnp.float32)
        for c in range(CHUNKS):
            copies[k, c].wait()
            piece = piece + jnp.dot(
                voxels[:, c * depth : (c + 1) * depth],
                held[k, c * depth : (c + 1) * depth, :],
                preferred_element_type=jnp.float32,
            )
        tile = jnp.concatenate([piece[:, i * LANES : (i + 1) * LANES] for i in range(8)], axis=0)
        low = lax.rem(starts[0, 0, k], WIN)
        tile = jnp.where(
            (lane & (WIN - 1)) >= low, pltpu.roll(tile, low, 1), pltpu.roll(tile, low + WIN, 1)
        )
        for q in range(4):
            tiles[q, 2 * k : 2 * k + 2, :] = tile[2 * q : 2 * q + 2, :]

    for q in range(4):
        full = jnp.where(row16 < 10, tiles[q], base)
        for b in range(16):
            sent[4 * b + q] = jnp.where(block_tile == b, code_tile, full).astype(jnp.bfloat16)


def derivative(x):
    row = lax.broadcasted_iota(jnp.int32, x.shape, 0) & 15
    lane = lane_iota(x.shape)

    def ahead(t):
        rolled = pltpu.roll(x, LANES - t, 1)
        after = jnp.where(row == 15, 0.0, pltpu.roll(rolled, x.shape[0] - 1, 0))
        return jnp.where(lane >= LANES - t, after, rolled)

    def behind(t):
        rolled = pltpu.roll(x, t, 1)
        before = jnp.where(row == 0, 0.0, pltpu.roll(rolled, 1, 0))
        return jnp.where(lane < t, before, rolled)

    return ((behind(2) - ahead(2)) + 8.0 * (ahead(1) - behind(1))) * (1.0 / 12.0)


def owner_kernel(got, spread, sent, residual, wide):
    wide[...] = got[...].astype(jnp.float32).reshape(OWNERS * ROWS, LANES)
    lane = lane_iota((OWNERS, LANES))
    low_half = lane < WIN
    within = (lane & (WIN - 1)).astype(jnp.float32)
    slot = jnp.where(low_half, lane & 31, 0).astype(jnp.float32)
    places, strips, later = [], [], []
    for k in range(K_MAX):
        info = wide[pl.ds(10 + k, OWNERS, stride=ROWS), :]
        turned = pltpu.roll(info, WIN, 1)
        code = jnp.where(low_half, info, turned)
        low = jnp.where(low_half, turned, info)
        following = jnp.where(code >= 16.0, code - 15.0, code + 16.0)
        wanted = jnp.where(lane < 32, code, following)
        places.append(jnp.where(low_half & (wanted == slot), 1.0, 0.0))
        first = within >= low
        later.append(first)
        parts = []
        for u in range(2):
            strip = wide[pl.ds(2 * k + u, OWNERS, stride=ROWS), :]
            parts.append((jnp.where(first, strip, 0.0), jnp.where(first, 0.0, strip)))
        strips.append(
            jnp.concatenate([parts[0][0], parts[1][0], parts[0][1], parts[1][1]], axis=1)
        )
    place = jnp.concatenate(places, axis=0).astype(jnp.bfloat16)
    strip = jnp.concatenate(strips, axis=0).astype(jnp.bfloat16)
    both = lax.dot_general(
        place, strip, (((0,), (0,)), ((), ())), preferred_element_type=jnp.float32
    )
    summed = both[0:32, 0:256] + both[32:64, 256:512]
    lane16 = lane_iota((16, LANES)) < WIN
    rows = []
    for u in range(2):
        even = summed[0:16, u * LANES : (u + 1) * LANES]
        odd = summed[16:32, u * LANES : (u + 1) * LANES]
        rows.append(jnp.where(lane16, even, pltpu.roll(odd, WIN, 1)))
        rows.append(jnp.where(lane16, pltpu.roll(even, WIN, 1), odd))
    signals = jnp.concatenate(rows, axis=0)
    resid = derivative(signals) - spread[...]
    adjoint = -derivative(resid)
    packed = []
    for u in range(2):
        a = adjoint[32 * u : 32 * u + 16]
        b = adjoint[32 * u + 16 : 32 * u + 32]
        packed.append(
            (
                jnp.where(lane16, a, pltpu.roll(b, WIN, 1)),
                jnp.where(lane16, pltpu.roll(a, WIN, 1), b),
            )
        )
    table = jnp.concatenate(
        [jnp.concatenate([packed[0][p], packed[1][p]], axis=1) for p in range(2)], axis=0
    )
    zero = jnp.zeros_like(table)
    table = jnp.concatenate(
        [
            jnp.concatenate([table, zero], axis=1),
            jnp.concatenate([zero, table], axis=1),
            jnp.zeros((64, 512), jnp.float32),
        ],
        axis=0,
    ).astype(jnp.bfloat16)
    cut = jnp.dot(place, table, preferred_element_type=jnp.float32)
    for k in range(K_MAX):
        mine = cut[k * OWNERS : (k + 1) * OWNERS]
        for u in range(2):
            window = jnp.where(
                later[k],
                mine[:, u * LANES : (u + 1) * LANES],
                mine[:, 256 + u * LANES : 256 + (u + 1) * LANES],
            )
            wide[pl.ds(2 * k + u, OWNERS, stride=ROWS), :] = window
    sent[...] = wide[...].reshape(OWNERS, ROWS, LANES).astype(jnp.bfloat16)
    for r in range(4):
        for h in range(16):
            residual[0, r : r + 1, h * LANES : (h + 1) * LANES] = resid[
                r * 16 + h : r * 16 + h + 1, :
            ]


def total_variation(image, before, after, is_first, is_last):
    lane = lane_iota((2, 512))
    row = lax.broadcasted_iota(jnp.int32, (2, 512), 0)

    def units(here, ahead, no_step):
        step_z = jnp.where(no_step, 0.0, ahead - here)
        step_y = jnp.where(row == 1, 0.0, pltpu.roll(here, 1, 0) - here)
        step_x = jnp.where(lane == 511, 0.0, pltpu.roll(here, 511, 1) - here)
        magnitude = jnp.sqrt(step_z * step_z + step_y * step_y + step_x * step_x + TV_EPS)
        return step_z / magnitude, step_y / magnitude, step_x / magnitude

    unit_z, unit_y, unit_x = units(image, after, is_last)
    below_z, _, _ = units(before, image, is_first)
    result = below_z - unit_z
    result = result + (jnp.where(row == 0, 0.0, pltpu.roll(unit_y, 1, 0)) - unit_y)
    return result + (jnp.where(lane == 0, 0.0, pltpu.roll(unit_x, 1, 1)) - unit_x)


def backward_kernel(
    ids, starts, counts, got, weights, image, before, after, grad, base, held, wins, sems
):
    depth = VOXELS // CHUNKS
    copies = {}
    for k in range(K_MAX):
        for c in range(CHUNKS):
            span = pl.ds(c * depth, depth)
            copies[k, c] = pltpu.make_async_copy(
                weights.at[0, 0, k, span], held.at[k, span], sems.at[k * CHUNKS + c]
            )
            copies[k, c].start()
    vox = lax.axis_index(VOX)
    here = image[0]
    tv = total_variation(here, before[0], after[0], vox == 0, vox == OWNERS - 1)
    base[0] = here - (STEP_SIZE * TV_WEIGHT) * tv

    live = counts[0, 0]
    lane = lane_iota((8, LANES))
    vectors = []
    for k in range(K_MAX):
        block = ids[0, 0, k]
        for q in range(4):
            strip = got[4 * block + q].astype(jnp.float32)
            wins[2 * q : 2 * q + 2, :] = strip[2 * k : 2 * k + 2, :]
        low = lax.rem(starts[0, 0, k], WIN)
        tile = wins[...]
        tile = jnp.where(
            (lane & (WIN - 1)) < WIN - low,
            pltpu.roll(tile, lax.rem(LANES - low, LANES), 1),
            pltpu.roll(tile, WIN - low, 1),
        )
        tile = jnp.where(k < live, tile, 0.0)
        vectors.append(
            jnp.concatenate([tile[i : i + 1, :] for i in range(8)], axis=1).astype(jnp.bfloat16)
        )
    for c in range(CHUNKS):
        total = jnp.zeros((1, depth), jnp.float32)
        for k in range(K_MAX):
            copies[k, c].wait()
            total = total + lax.dot_general(
                vectors[k],
                held[k, c * depth : (c + 1) * depth, :],
                (((1,), (1,)), ((), ())),
                preferred_element_type=jnp.float32,
            )
        grad[0, c : c + 1, :] = total


def smem():
    return pl.BlockSpec(memory_space=pltpu.SMEM)


def vmem():
    return pl.BlockSpec(memory_space=pltpu.VMEM)


def anywhere():
    return pl.BlockSpec(memory_space=pl.ANY)


def held_scratch():
    return pltpu.VMEM((K_MAX, VOXELS, CELLS), jnp.bfloat16)


def on_device(image, weights, block_ids, offsets, counts, measured):
    before = lax.ppermute(image, VOX, [(i, i + 1) for i in range(OWNERS - 1)])
    after = lax.ppermute(image, VOX, [(i + 1, i) for i in range(OWNERS - 1)])
    sent, spread = pl.pallas_call(
        forward_kernel,
        out_shape=(
            jax.ShapeDtypeStruct((OWNERS, ROWS, LANES), jnp.bfloat16),
            jax.ShapeDtypeStruct((64, LANES), jnp.float32),
        ),
        in_specs=[smem(), smem(), smem(), vmem(), anywhere(), vmem()],
        out_specs=(vmem(), vmem()),
        scratch_shapes=[
            held_scratch(),
            pltpu.VMEM((4, ROWS, LANES), jnp.float32),
            pltpu.SemaphoreType.DMA((K_MAX * CHUNKS,)),
        ],
        compiler_params=pltpu.CompilerParams(vmem_limit_bytes=40 * MIB),
        name="forward",
    )(block_ids, offsets, counts, image, weights, measured)
    got = lax.all_to_all(sent, VOX, 0, 0, tiled=True)
    sent, residual = pl.pallas_call(
        owner_kernel,
        out_shape=(
            jax.ShapeDtypeStruct((OWNERS, ROWS, LANES), jnp.bfloat16),
            jax.ShapeDtypeStruct((1, 4, 2048), jnp.float32),
        ),
        in_specs=[vmem(), vmem()],
        out_specs=(vmem(), vmem()),
        scratch_shapes=[pltpu.VMEM((OWNERS * ROWS, LANES), jnp.float32)],
        compiler_params=pltpu.CompilerParams(vmem_limit_bytes=40 * MIB),
        name="owner",
    )(got, spread)
    got = lax.all_to_all(sent, VOX, 0, 0, tiled=True)
    grad, base = pl.pallas_call(
        backward_kernel,
        out_shape=(
            jax.ShapeDtypeStruct((1, 2, 512), jnp.float32),
            jax.ShapeDtypeStruct((1, 2, 512), jnp.float32),
        ),
        in_specs=[smem(), smem(), smem(), vmem(), anywhere(), vmem(), vmem(), vmem()],
        out_specs=(vmem(), vmem()),
        scratch_shapes=[
            held_scratch(),
            pltpu.VMEM((8, LANES), jnp.float32),
            pltpu.SemaphoreType.DMA((K_MAX * CHUNKS,)),
        ],
        compiler_params=pltpu.CompilerParams(vmem_limit_bytes=40 * MIB),
        name="backward",
    )(block_ids, offsets, counts, got, weights, image, before, after)
    grad = grad + lax.ppermute(grad, "core", [(0, 1), (1, 0)])
    grad = grad + lax.ppermute(grad, "z_hi", [(0, 1), (1, 0)])
    return (base - STEP_SIZE * grad, residual)


def solution(mesh):
    fine = Mesh(mesh.devices.reshape(4, 4, 4, 2, 2), VOX + SEN)
    placed = (
        P(VOX, None, None),
        P(VOX, SEN, None, None, None),
        P(VOX, SEN, None),
        P(VOX, SEN, None),
        P(VOX, SEN),
        P(SEN, VOX, None),
    )
    return jax.shard_map(
        on_device,
        mesh=fine,
        in_specs=placed,
        out_specs=(P(VOX, None, None), P(SEN, VOX, None)),
        check_vma=False,
    )
```

time: 1130 us -> 74.4 us (0.07)
  waiting for transfers between devices: 996 us -> 8.99 us
  blocking collectives: 54.1 us -> 23.3 us
  local copies, waits for them, and re-layouts: 24.4 us -> 10.7 us
  between operations: 14.8 us -> 1.39 us
  starting transfers between devices: 5.74 us -> 18.4 us
  matrix products: 12.3 us -> 0 us
    psum x1 -> x0, waiting for transfers between devices: 719 us -> none  [on_device(): summed = lax.psum(partial_value[None], 'vox')]
    all_gather x1 -> x0, waiting for transfers between devices: 273 us -> none  [on_device(): whole_measured = lax.all_gather(measured, 'vox', axis=1, tiled=True)]
    psum x1 -> x0, blocking collectives: 54.1 us -> none  [on_device(): backprojected = lax.psum(grad_local, 'sen').reshape(image.shape)]
    all_to_all x0 -> x1, blocking collectives: none -> 23.3 us  [on_device(): got = lax.all_to_all(sent, VOX, 0, 0, tiled=True)]
    dot_general x2 -> x0, matrix products: 12.3 us -> none  [the longest x1 6.8 us: on_device(): jnp.einsum('kc,kvc->v', windows, blocks, preferred_element_type=jnp.float32)]
  transfers between devices with their start and end apart: 4 -> 5, of which waited for: 3 -> 4; matrix products, arithmetic and copies ran while one was open for 2% -> 0% of each run, Pallas kernels for 0% -> 0%
where the time goes in v1:
time: 74.4 us; the launch traced here: 74 us
  blocking collectives  23.3 us (31%)
  starting transfers between devices  18.4 us (25%)
  local copies, waits for them, and re-layouts  10.7 us (14%)
  Pallas kernels  10.6 us (14%)
  waiting for transfers between devices  8.99 us (12%)
  between operations  1.39 us (2%)
    all_to_all x1, blocking collectives, on_device(): got = lax.all_to_all(sent, VOX, 0, 0, tiled=True)  23.3 us
    unnamed x18, local copies, waits for them, and re-layouts  10.7 us
    all_to_all x1, starting transfers between devices, on_device(): got = lax.all_to_all(sent, VOX, 0, 0, tiled=True)  6.27 us
    pallas_call x1, Pallas kernels, on_device(): pl.pallas_call(backward_kernel, out_shape=(jax.ShapeDtypeStruct((1, 2, 51...  4.62 us
    ppermute x1, starting transfers between devices, on_device(): grad = grad + lax.ppermute(grad, 'z_hi', [(0, 1), (1, 0)])  4.21 us
    pallas_call x1, Pallas kernels, on_device(): pl.pallas_call(forward_kernel, out_shape=(jax.ShapeDtypeStruct((OWNERS, R...  4.11 us
    ppermute x1, starting transfers between devices, on_device(): grad = grad + lax.ppermute(grad, 'core', [(0, 1), (1, 0)])  3.67 us
    ppermute x1, waiting for transfers between devices, on_device(): after = lax.ppermute(image, VOX, [(i + 1, i) for i in range(OWNERS - 1)])  3.38 us
  transfers between devices with their start and end apart: 5, of which 4 were waited for; matrix products, arithmetic and copies ran while one was open for 0% of the time, Pallas kernels for 0%

profile of v1, /device:TPU:1, one launch (start us, length us, event | category | flops | bytes accessed | tf_op | source)
XLA Modules:
  0.0 74.0 jit_solution(9981317888605980529)
XLA Ops:
  0.6 0.0 copy-start.6
  0.6 0.0 copy-start.8
  1.3 0.0 copy-start
  1.3 4.0 %copy-done = bf16[1,1,5,1024,1024]{4,3,2,1,0:T(8,128)(2,1)S(1)} copy-done((bf16[1,1,5,1024,1024]{4,3,2,1,0:T(8,128)(2,1)S(1)}, bf16[1,1,5,1024,1024]{4,3,2,1,0:T(8,128)(2,1)}, u32[]{:S(2)}) %copy-start) | copy-done | bytes 10485784
  5.3 0.0 copy-start.2
  5.3 0.7 copy-done.2
  6.0 0.0 copy-start.4
  6.0 0.7 copy-done.4
  6.7 0.0 copy-start.5
  6.7 0.7 copy-done.5
  7.4 0.0 copy-start.7
  7.4 0.7 copy-done.7
  8.0 0.0 copy-start.3
  8.0 4.1 %forward.1 = (bf16[64,16,128]{2,1,0:T(8,128)(2,1)S(1)}, f32[64,128]{1,0:T(8,128)S(1)}) custom-call(s32[1,1,5]{2,1,0:T(1,128)S(1)} %copy-done.5, s32[1,1,5]{2,1,0:T(1,128)S(1)} %copy-done.7, s32[1,1]{1,0:T(1,128)S(6)} %copy.8.counts, f32[1,2,512]{2,1,0:T(2,128)S(1)} %copy-done.2, bf16[1,1,5,1024,1024]{4,3,2,1,0:T(8,128)(2,1)S(1)} %copy-done, ...), custom_call_target="tpu_custom_call" | custom-call | tf_op jit(solution)/shard_map/forward/pallas_call | solution.py:275
  12.2 23.3 %all_to_all.10.got = bf16[64,16,128]{2,1,0:T(8,128)(2,1)S(1)} all-to-all(bf16[64,16,128]{2,1,0:T(8,128)(2,1)S(1)} %get-tuple-element.8), channel_id=1, replica_groups=mesh['y'=4,'x'=4,'z_lo'=4,'z_hi'=2,'core'=2] {'y','x','z_lo'}, dimensions={0} | all-to-all | bytes 524288 | tf_op jit(solution)/shard_map/all_to_all | solution.py:291
  35.5 1.8 %owner.1 = (bf16[64,16,128]{2,1,0:T(8,128)(2,1)}, f32[1,4,2048]{2,1,0:T(4,128)}) custom-call(bf16[64,16,128]{2,1,0:T(8,128)(2,1)S(1)} %all_to_all.10.got, f32[64,128]{1,0:T(8,128)S(1)} %get-tuple-element.9.spread), custom_call_target="tpu_custom_call" | custom-call | tf_op jit(solution)/shard_map/owner/pallas_call | solution.py:292
  37.3 6.3 %all-to-all-start.1 = ((bf16[64,16,128]{2,1,0:T(8,128)(2,1)}), bf16[64,16,128]{2,1,0:T(8,128)(2,1)S(1)}, u32[]{:S(2)}, u32[]{:S(2)}) async-start(bf16[64,16,128]{2,1,0:T(8,128)(2,1)} %get-tuple-element.10), calls=%async_computation.1 | async-start | bytes 524288 | tf_op jit(solution)/shard_map/all_to_all | solution.py:304
  43.6 0.0 copy-done.3
  43.6 2.9 %collective-permute-start = (f32[1,2,512]{2,1,0:T(2,128)S(1)}, f32[1,2,512]{2,1,0:T(2,128)S(1)}, u32[]{:S(2)}, u32[]{:S(2)}) collective-permute-start(f32[1,2,512]{2,1,0:T(2,128)S(1)} %copy-done.3), channel_id=1, source_target_pairs={{0,4},{4,8},{8,12},{12,16},{16,20},{20,24},{24,28},{28,32},{32,36}... | collective-permute-start | bytes 12296 | tf_op jit(solution)/shard_map/ppermute | solution.py:273
  46.5 1.3 %collective-permute-start.1 = (f32[1,2,512]{2,1,0:T(2,128)S(1)}, f32[1,2,512]{2,1,0:T(2,128)S(1)}, u32[]{:S(2)}, u32[]{:S(2)}) collective-permute-start(f32[1,2,512]{2,1,0:T(2,128)S(1)} %copy-done.3), channel_id=1, source_target_pairs={{4,0},{8,4},{12,8},{16,12},{20,16},{24,20},{28,24},{32,28},{36,32}... | collective-permute-start | bytes 12296 | tf_op jit(solution)/shard_map/ppermute | solution.py:274
  47.8 0.0 collective-permute-done.before
  47.8 3.4 %collective-permute-done.1.after = f32[1,2,512]{2,1,0:T(2,128)S(1)} collective-permute-done((f32[1,2,512]{2,1,0:T(2,128)S(1)}, f32[1,2,512]{2,1,0:T(2,128)S(1)}, u32[]{:S(2)}, u32[]{:S(2)}) %collective-permute-start.1) | collective-permute-done | bytes 4128 | tf_op jit(solution)/shard_map/ppermute | solution.py:274
  51.2 2.6 %all-to-all-done.1.got = bf16[64,16,128]{2,1,0:T(8,128)(2,1)S(1)} async-done(((bf16[64,16,128]{2,1,0:T(8,128)(2,1)}), bf16[64,16,128]{2,1,0:T(8,128)(2,1)S(1)}, u32[]{:S(2)}, u32[]{:S(2)}) %all-to-all-start.1) | async-done | bytes 262176 | tf_op jit(solution)/shard_map/all_to_all | solution.py:304
  53.9 0.0 copy-done.6
  53.9 0.0 copy-done.8
  53.9 0.0 copy-start.1
  53.9 4.0 %copy-done.1 = bf16[1,1,5,1024,1024]{4,3,2,1,0:T(8,128)(2,1)S(1)} copy-done((bf16[1,1,5,1024,1024]{4,3,2,1,0:T(8,128)(2,1)S(1)}, bf16[1,1,5,1024,1024]{4,3,2,1,0:T(8,128)(2,1)}, u32[]{:S(2)}) %copy-start.1) | copy-done | bytes 10485784
  57.9 4.6 %backward.1 = (f32[1,2,512]{2,1,0:T(2,128)S(1)}, f32[1,2,512]{2,1,0:T(2,128)S(1)}) custom-call(s32[1,1,5]{2,1,0:T(1,128)S(1)} %copy-done.6, s32[1,1,5]{2,1,0:T(1,128)S(1)} %copy-done.8, s32[1,1]{1,0:T(1,128)S(6)} %copy.8.counts, bf16[64,16,128]{2,1,0:T(8,128)(2,1)S(1)} %all-to-all-done.1.got, bf16[1,1,5,1024,1024]{4,3,2,1,0:T(8,128)(2,1)S(1)} %copy-done.1, ...), custom_call_target="tpu_custom_call" | custom-call | tf_op jit(solution)/shard_map/backward/pallas_call | solution.py:305
  62.5 3.7 %collective-permute-start.2 = (f32[1,2,512]{2,1,0:T(2,128)S(1)}, f32[1,2,512]{2,1,0:T(2,128)S(1)}, u32[]{:S(2)}, u32[]{:S(2)}) collective-permute-start(f32[1,2,512]{2,1,0:T(2,128)S(1)} %get-tuple-element.12), channel_id=1, source_target_pairs={{0,1},{1,0},{2,3},{3,2},{4,5},{5,4},{6,7},{7,6},{8,9},{9,8},{10,11... | collective-permute-start | bytes 12296 | tf_op jit(solution)/shard_map/ppermute | solution.py:321
  66.2 0.8 %collective-permute-done.2 = f32[1,2,512]{2,1,0:T(2,128)S(1)} collective-permute-done((f32[1,2,512]{2,1,0:T(2,128)S(1)}, f32[1,2,512]{2,1,0:T(2,128)S(1)}, u32[]{:S(2)}, u32[]{:S(2)}) %collective-permute-start.2) | collective-permute-done | bytes 4128 | tf_op jit(solution)/shard_map/ppermute | solution.py:321
  67.0 4.2 %collective-permute-start.3 = (f32[1,2,512]{2,1,0:T(2,128)S(1)}, f32[1,2,512]{2,1,0:T(2,128)S(1)}, u32[]{:S(2)}, u32[]{:S(2)}) collective-permute-start(f32[1,2,512]{2,1,0:T(2,128)S(1)} %add.6), channel_id=1, source_target_pairs={{0,2},{2,0},{1,3},{3,1},{4,6},{6,4},{5,7},{7,5},{8,10},{10,8},{9,1... | collective-permute-start | bytes 12296 | tf_op jit(solution)/shard_map/ppermute | solution.py:322
  71.2 2.1 %collective-permute-done.3 = f32[1,2,512]{2,1,0:T(2,128)S(1)} collective-permute-done((f32[1,2,512]{2,1,0:T(2,128)S(1)}, f32[1,2,512]{2,1,0:T(2,128)S(1)}, u32[]{:S(2)}, u32[]{:S(2)}) %collective-permute-start.3) | collective-permute-done | bytes 4128 | tf_op jit(solution)/shard_map/ppermute | solution.py:322
  73.4 0.6 multiply_subtract_fusion
  (1 shorter events, 0.0 us)
Async XLA Ops:
  0.6 53.2 %copy-start.6 = (s32[1,1,5]{2,1,0:T(1,128)S(1)}, s32[1,1,5]{2,1,0:T(1,128)}, u32[]{:S(2)}) copy-start(s32[1,1,5]{2,1,0:T(1,128)} %ids.3) | copy-start | bytes 64
  0.6 53.2 %copy-start.8 = (s32[1,1,5]{2,1,0:T(1,128)S(1)}, s32[1,1,5]{2,1,0:T(1,128)}, u32[]{:S(2)}) copy-start(s32[1,1,5]{2,1,0:T(1,128)} %starts.3) | copy-start | bytes 64
  1.3 4.0 %copy-start = (bf16[1,1,5,1024,1024]{4,3,2,1,0:T(8,128)(2,1)S(1)}, bf16[1,1,5,1024,1024]{4,3,2,1,0:T(8,128)(2,1)}, u32[]{:S(2)}) copy-start(bf16[1,1,5,1024,1024]{4,3,2,1,0:T(8,128)(2,1)} %weights.3) | copy-start | bytes 31457284
  5.3 0.7 copy-start.2
  6.0 0.7 copy-start.4
  6.7 0.7 copy-start.5
  7.4 0.7 copy-start.7
  8.0 35.6 %copy-start.3 = (f32[1,2,512]{2,1,0:T(2,128)S(1)}, f32[1,2,512]{2,1,0:T(2,128)}, u32[]{:S(2)}) copy-start(f32[1,2,512]{2,1,0:T(2,128)} %image.3) | copy-start | bytes 12292
  37.3 16.5 %all-to-all-start.1 = ((bf16[64,16,128]{2,1,0:T(8,128)(2,1)}), bf16[64,16,128]{2,1,0:T(8,128)(2,1)S(1)}, u32[]{:S(2)}, u32[]{:S(2)}) async-start(bf16[64,16,128]{2,1,0:T(8,128)(2,1)} %get-tuple-element.10), calls=%async_computation.1 | async-start | bytes 524288 | tf_op jit(solution)/shard_map/all_to_all | solution.py:304
  43.6 4.2 %collective-permute-start = (f32[1,2,512]{2,1,0:T(2,128)S(1)}, f32[1,2,512]{2,1,0:T(2,128)S(1)}, u32[]{:S(2)}, u32[]{:S(2)}) collective-permute-start(f32[1,2,512]{2,1,0:T(2,128)S(1)} %copy-done.3), channel_id=1, source_target_pairs={{0,4},{4,8},{8,12},{12,16},{16,20},{20,24},{24,28},{28,32},{32,36}... | collective-permute-start | bytes 12296 | tf_op jit(solution)/shard_map/ppermute | solution.py:273
  46.5 4.7 %collective-permute-start.1 = (f32[1,2,512]{2,1,0:T(2,128)S(1)}, f32[1,2,512]{2,1,0:T(2,128)S(1)}, u32[]{:S(2)}, u32[]{:S(2)}) collective-permute-start(f32[1,2,512]{2,1,0:T(2,128)S(1)} %copy-done.3), channel_id=1, source_target_pairs={{4,0},{8,4},{12,8},{16,12},{20,16},{24,20},{28,24},{32,28},{36,32}... | collective-permute-start | bytes 12296 | tf_op jit(solution)/shard_map/ppermute | solution.py:274
  53.9 4.0 %copy-start.1 = (bf16[1,1,5,1024,1024]{4,3,2,1,0:T(8,128)(2,1)S(1)}, bf16[1,1,5,1024,1024]{4,3,2,1,0:T(8,128)(2,1)}, u32[]{:S(2)}) copy-start(bf16[1,1,5,1024,1024]{4,3,2,1,0:T(8,128)(2,1)} %weights.3) | copy-start | bytes 31457284
  62.5 4.5 %collective-permute-start.2 = (f32[1,2,512]{2,1,0:T(2,128)S(1)}, f32[1,2,512]{2,1,0:T(2,128)S(1)}, u32[]{:S(2)}, u32[]{:S(2)}) collective-permute-start(f32[1,2,512]{2,1,0:T(2,128)S(1)} %get-tuple-element.12), channel_id=1, source_target_pairs={{0,1},{1,0},{2,3},{3,2},{4,5},{5,4},{6,7},{7,6},{8,9},{9,8},{10,11... | collective-permute-start | bytes 12296 | tf_op jit(solution)/shard_map/ppermute | solution.py:321
  67.0 6.4 %collective-permute-start.3 = (f32[1,2,512]{2,1,0:T(2,128)S(1)}, f32[1,2,512]{2,1,0:T(2,128)S(1)}, u32[]{:S(2)}, u32[]{:S(2)}) collective-permute-start(f32[1,2,512]{2,1,0:T(2,128)S(1)} %add.6), channel_id=1, source_target_pairs={{0,2},{2,0},{1,3},{3,1},{4,6},{6,4},{5,7},{7,5},{8,10},{10,8},{9,1... | collective-permute-start | bytes 12296 | tf_op jit(solution)/shard_map/ppermute | solution.py:322

commit v2 on v1

--- a/solution.py
+++ b/solution.py
@@ -31,7 +31,50 @@
     return lax.broadcasted_iota(jnp.int32, shape, len(shape) - 1)
 
 
-def forward_kernel(ids, starts, counts, image, weights, measured, sent, spread, held, tiles, sems):
+def as_tile(image):
+    rows = [image[0, y : y + 1, t * LANES : (t + 1) * LANES] for y in range(2) for t in range(4)]
+    return jnp.concatenate(rows, axis=0)
+
+
+def split_three(x):
+    parts = []
+    for _ in range(3):
+        part = x.astype(jnp.bfloat16).astype(jnp.float32)
+        parts.append(part)
+        x = x - part
+    return parts
+
+
+def forward_kernel(
+    ids_hbm,
+    starts_hbm,
+    counts,
+    image_hbm,
+    weights,
+    measured_hbm,
+    sent,
+    spread,
+    held,
+    ids,
+    starts,
+    image,
+    measured,
+    tiles,
+    halo,
+    small_sems,
+    sems,
+):
+    small = []
+    for i, (src, dst) in enumerate(
+        (
+            (image_hbm, image),
+            (ids_hbm, ids),
+            (starts_hbm, starts),
+            (measured_hbm, measured),
+        )
+    ):
+        small.append(pltpu.make_async_copy(src, dst, small_sems.at[i]))
+        small[-1].start()
     depth = VOXELS // CHUNKS
     copies = {}
     for k in range(K_MAX):
@@ -41,19 +84,24 @@
                 weights.at[0, 0, k, span], held.at[k, span], sems.at[k * CHUNKS + c]
             )
             copies[k, c].start()
+    for copy in small:
+        copy.wait()
 
     own = measured[0].astype(jnp.float32)
     for r in range(4):
         for h in range(16):
             spread[r * 16 + h : r * 16 + h + 1, :] = own[r : r + 1, h * LANES : (h + 1) * LANES]
 
+    plane = as_tile(image)
+    turned = jnp.concatenate(split_three(plane) + [jnp.zeros((104, LANES), jnp.float32)], axis=0).T
+    halo[...] = turned[0:64] + pltpu.roll(turned[64:128], 24, 1)
+
     voxels = jnp.concatenate([image[0, 0:1, :], image[0, 1:2, :]], axis=1).astype(jnp.bfloat16)
     lane = lane_iota((8, LANES))
-    row16 = lax.broadcasted_iota(jnp.int32, (ROWS, LANES), 0)
-    lane16 = lane_iota((ROWS, LANES))
-    base = jnp.full((ROWS, LANES), NOWHERE, jnp.float32)
-    code_tile = jnp.full((ROWS, LANES), NOWHERE, jnp.float32)
-    block_tile = jnp.full((ROWS, LANES), -1, jnp.int32)
+    row = lax.broadcasted_iota(jnp.int32, (8, LANES), 0)
+    base = jnp.full((8, LANES), NOWHERE, jnp.float32)
+    code_tile = jnp.full((8, LANES), NOWHERE, jnp.float32)
+    block_tile = jnp.full((8, LANES), -1, jnp.int32)
     live = counts[0, 0]
     for k in range(K_MAX):
         start = starts[0, 0, k]
@@ -61,10 +109,10 @@
         low = start - coarse * WIN
         code = (coarse & 1) * 16 + (coarse >> 1)
         block = jnp.where(k < live, ids[0, 0, k], -1)
-        here = row16 == 10 + k
-        base = jnp.where(here & (lane16 >= WIN), low.astype(jnp.float32), base)
-        code_tile = jnp.where(here & (lane16 < WIN), code.astype(jnp.float32), code_tile)
-        block_tile = jnp.where(here & (lane16 < WIN), block, block_tile)
+        here = row == 2 + k
+        base = jnp.where(here & (lane >= WIN), low.astype(jnp.float32), base)
+        code_tile = jnp.where(here & (lane < WIN), code.astype(jnp.float32), code_tile)
+        block_tile = jnp.where(here & (lane < WIN), block, block_tile)
 
     for k in range(K_MAX):
         piece = jnp.zeros((1, CELLS), jnp.float32)
@@ -82,11 +130,18 @@
         )
         for q in range(4):
             tiles[q, 2 * k : 2 * k + 2, :] = tile[2 * q : 2 * q + 2, :]
+        if k == 3:
+            for q in range(4):
+                data = tiles[q, 0:8, :].astype(jnp.bfloat16)
+                for b in range(16):
+                    sent[4 * b + q, 0:8, :] = data
 
     for q in range(4):
-        full = jnp.where(row16 < 10, tiles[q], base)
+        full = jnp.where(row < 2, tiles[q, 8:16, :], base)
         for b in range(16):
-            sent[4 * b + q] = jnp.where(block_tile == b, code_tile, full).astype(jnp.bfloat16)
+            own_halo = jnp.broadcast_to(halo[4 * b + q : 4 * b + q + 1, :], (8, LANES))
+            marked = jnp.where(block_tile == b, code_tile, full)
+            sent[4 * b + q, 8:16, :] = jnp.where(row == 7, own_halo, marked).astype(jnp.bfloat16)
 
 
 def derivative(x):
@@ -178,6 +233,12 @@
                 mine[:, 256 + u * LANES : 256 + (u + 1) * LANES],
             )
             wide[pl.ds(2 * k + u, OWNERS, stride=ROWS), :] = window
+    shard = wide[pl.ds(15, OWNERS, stride=ROWS), :]
+    wide[pl.ds(10, OWNERS, stride=ROWS), :] = jnp.where(
+        low_half,
+        pltpu.roll(shard, 1, 0),
+        pltpu.roll(pltpu.roll(shard, OWNERS - 1, 0), WIN, 1),
+    )
     sent[...] = wide[...].reshape(OWNERS, ROWS, LANES).astype(jnp.bfloat16)
     for r in range(4):
         for h in range(16):
@@ -187,40 +248,45 @@
 
 
 def total_variation(image, before, after, is_first, is_last):
-    lane = lane_iota((2, 512))
-    row = lax.broadcasted_iota(jnp.int32, (2, 512), 0)
+    lane = lane_iota((8, LANES))
+    row = lax.broadcasted_iota(jnp.int32, (8, LANES), 0)
+    last_x = (lane == LANES - 1) & ((row & 3) == 3)
+    first_x = (lane == 0) & ((row & 3) == 0)
 
     def units(here, ahead, no_step):
         step_z = jnp.where(no_step, 0.0, ahead - here)
-        step_y = jnp.where(row == 1, 0.0, pltpu.roll(here, 1, 0) - here)
-        step_x = jnp.where(lane == 511, 0.0, pltpu.roll(here, 511, 1) - here)
+        step_y = jnp.where(row >= 4, 0.0, pltpu.roll(here, 4, 0) - here)
+        moved = pltpu.roll(here, LANES - 1, 1)
+        moved = jnp.where(lane == LANES - 1, pltpu.roll(moved, 7, 0), moved)
+        step_x = jnp.where(last_x, 0.0, moved - here)
         magnitude = jnp.sqrt(step_z * step_z + step_y * step_y + step_x * step_x + TV_EPS)
         return step_z / magnitude, step_y / magnitude, step_x / magnitude
 
     unit_z, unit_y, unit_x = units(image, after, is_last)
     below_z, _, _ = units(before, image, is_first)
     result = below_z - unit_z
-    result = result + (jnp.where(row == 0, 0.0, pltpu.roll(unit_y, 1, 0)) - unit_y)
-    return result + (jnp.where(lane == 0, 0.0, pltpu.roll(unit_x, 1, 1)) - unit_x)
-
-
-def backward_kernel(
-    ids, starts, counts, got, weights, image, before, after, grad, base, held, wins, sems
-):
-    depth = VOXELS // CHUNKS
-    copies = {}
-    for k in range(K_MAX):
-        for c in range(CHUNKS):
-            span = pl.ds(c * depth, depth)
-            copies[k, c] = pltpu.make_async_copy(
-                weights.at[0, 0, k, span], held.at[k, span], sems.at[k * CHUNKS + c]
-            )
-            copies[k, c].start()
+    result = result + (jnp.where(row < 4, 0.0, pltpu.roll(unit_y, 4, 0)) - unit_y)
+    moved = pltpu.roll(unit_x, 1, 1)
+    moved = jnp.where(lane == 0, pltpu.roll(moved, 1, 0), moved)
+    return result + (jnp.where(first_x, 0.0, moved) - unit_x)
+
+
+def smooth_kernel(got, image, base, wide):
     vox = lax.axis_index(VOX)
-    here = image[0]
-    tv = total_variation(here, before[0], after[0], vox == 0, vox == OWNERS - 1)
-    base[0] = here - (STEP_SIZE * TV_WEIGHT) * tv
-
+    wide[...] = got[:, 8:16, :].astype(jnp.float32).reshape(OWNERS * 8, LANES)
+    shard = wide[pl.ds(2, OWNERS, stride=8), :]
+    whole = shard + (pltpu.roll(shard, LANES - 8, 1) + pltpu.roll(shard, LANES - 16, 1))
+    turned = jnp.concatenate([whole, pltpu.roll(whole, LANES - 24, 1)], axis=0).T
+    here = as_tile(image)
+    tv = total_variation(here, turned[0:8], turned[64:72], vox == 0, vox == OWNERS - 1)
+    out = here - (STEP_SIZE * TV_WEIGHT) * tv
+    for y in range(2):
+        for t in range(4):
+            base[0, y : y + 1, t * LANES : (t + 1) * LANES] = out[y * 4 + t : y * 4 + t + 1]
+
+
+def backward_kernel(ids, starts, counts, got, held, grad, wins):
+    depth = VOXELS // 2
     live = counts[0, 0]
     lane = lane_iota((8, LANES))
     vectors = []
@@ -240,10 +306,9 @@
         vectors.append(
             jnp.concatenate([tile[i : i + 1, :] for i in range(8)], axis=1).astype(jnp.bfloat16)
         )
-    for c in range(CHUNKS):
+    for c in range(2):
         total = jnp.zeros((1, depth), jnp.float32)
         for k in range(K_MAX):
-            copies[k, c].wait()
             total = total + lax.dot_general(
                 vectors[k],
                 held[k, c * depth : (c + 1) * depth, :],
@@ -261,33 +326,44 @@
     return pl.BlockSpec(memory_space=pltpu.VMEM)
 
 
-def anywhere():
-    return pl.BlockSpec(memory_space=pl.ANY)
-
-
-def held_scratch():
-    return pltpu.VMEM((K_MAX, VOXELS, CELLS), jnp.bfloat16)
+def hbm():
+    return pl.BlockSpec(memory_space=pltpu.HBM)
+
+
+def in_hbm(array):
+    return pltpu.with_memory_space_constraint(array, pltpu.HBM)
 
 
 def on_device(image, weights, block_ids, offsets, counts, measured):
-    before = lax.ppermute(image, VOX, [(i, i + 1) for i in range(OWNERS - 1)])
-    after = lax.ppermute(image, VOX, [(i + 1, i) for i in range(OWNERS - 1)])
-    sent, spread = pl.pallas_call(
+    sent, spread, held = pl.pallas_call(
         forward_kernel,
         out_shape=(
             jax.ShapeDtypeStruct((OWNERS, ROWS, LANES), jnp.bfloat16),
             jax.ShapeDtypeStruct((64, LANES), jnp.float32),
+            jax.ShapeDtypeStruct((K_MAX, VOXELS, CELLS), jnp.bfloat16),
         ),
-        in_specs=[smem(), smem(), smem(), vmem(), anywhere(), vmem()],
-        out_specs=(vmem(), vmem()),
+        in_specs=[hbm(), hbm(), smem(), hbm(), hbm(), hbm()],
+        out_specs=(vmem(), vmem(), vmem()),
         scratch_shapes=[
-            held_scratch(),
+            pltpu.SMEM((1, 1, K_MAX), jnp.int32),
+            pltpu.SMEM((1, 1, K_MAX), jnp.int32),
+            pltpu.VMEM((1, 2, 512), jnp.float32),
+            pltpu.VMEM((1, 4, 2048), jnp.bfloat16),
             pltpu.VMEM((4, ROWS, LANES), jnp.float32),
+            pltpu.VMEM((OWNERS, LANES), jnp.float32),
+            pltpu.SemaphoreType.DMA((4,)),
             pltpu.SemaphoreType.DMA((K_MAX * CHUNKS,)),
         ],
-        compiler_params=pltpu.CompilerParams(vmem_limit_bytes=40 * MIB),
+        compiler_params=pltpu.CompilerParams(vmem_limit_bytes=20 * MIB),
         name="forward",
-    )(block_ids, offsets, counts, image, weights, measured)
+    )(
+        in_hbm(block_ids),
+        in_hbm(offsets),
+        counts,
+        in_hbm(image),
+        in_hbm(weights),
+        in_hbm(measured),
+    )
     got = lax.all_to_all(sent, VOX, 0, 0, tiled=True)
     sent, residual = pl.pallas_call(
         owner_kernel,
@@ -298,29 +374,32 @@
         in_specs=[vmem(), vmem()],
         out_specs=(vmem(), vmem()),
         scratch_shapes=[pltpu.VMEM((OWNERS * ROWS, LANES), jnp.float32)],
-        compiler_params=pltpu.CompilerParams(vmem_limit_bytes=40 * MIB),
+        compiler_params=pltpu.CompilerParams(vmem_limit_bytes=8 * MIB),
         name="owner",
     )(got, spread)
     got = lax.all_to_all(sent, VOX, 0, 0, tiled=True)
-    grad, base = pl.pallas_call(
+    grad = pl.pallas_call(
         backward_kernel,
-        out_shape=(
-            jax.ShapeDtypeStruct((1, 2, 512), jnp.float32),
-            jax.ShapeDtypeStruct((1, 2, 512), jnp.float32),
-        ),
-        in_specs=[smem(), smem(), smem(), vmem(), anywhere(), vmem(), vmem(), vmem()],
-        out_specs=(vmem(), vmem()),
-        scratch_shapes=[
-            held_scratch(),
-            pltpu.VMEM((8, LANES), jnp.float32),
-            pltpu.SemaphoreType.DMA((K_MAX * CHUNKS,)),
-        ],
-        compiler_params=pltpu.CompilerParams(vmem_limit_bytes=40 * MIB),
+        out_shape=jax.ShapeDtypeStruct((1, 2, 512), jnp.float32),
+        in_specs=[smem(), smem(), smem(), vmem(), vmem()],
+        out_specs=vmem(),
+        scratch_shapes=[pltpu.VMEM((8, LANES), jnp.float32)],
+        compiler_params=pltpu.CompilerParams(vmem_limit_bytes=20 * MIB),
         name="backward",
-    )(block_ids, offsets, counts, got, weights, image, before, after)
+    )(block_ids, offsets, counts, got, held)
     grad = grad + lax.ppermute(grad, "core", [(0, 1), (1, 0)])
-    grad = grad + lax.ppermute(grad, "z_hi", [(0, 1), (1, 0)])
-    return (base - STEP_SIZE * grad, residual)
+    other = lax.ppermute(grad, "z_hi", [(0, 1), (1, 0)])
+    base = pl.pallas_call(
+        smooth_kernel,
+        out_shape=jax.ShapeDtypeStruct((1, 2, 512), jnp.float32),
+        in_specs=[vmem(), vmem()],
+        out_specs=vmem(),
+        scratch_shapes=[pltpu.VMEM((OWNERS * 8, LANES), jnp.float32)],
+        compiler_params=pltpu.CompilerParams(vmem_limit_bytes=8 * MIB),
+        cost_estimate=pl.CostEstimate(flops=100000, bytes_accessed=1 << 19, transcendentals=4096),
+        name="smooth",
+    )(got, image)
+    return (base - STEP_SIZE * (grad + other), residual)
 
 
 def solution(mesh):

time: 74.4 us -> 64.2 us (0.86)
  blocking collectives: 23.3 us -> 39.6 us
  local copies, waits for them, and re-layouts: 10.7 us -> 0.01 us
  starting transfers between devices: 18.4 us -> 7.73 us
  waiting for transfers between devices: 8.99 us -> 2.67 us
  Pallas kernels: 10.6 us -> 12.1 us
    all_to_all x1 -> x2, blocking collectives: 23.3 us -> 39.6 us  [on_device(): got = lax.all_to_all(sent, VOX, 0, 0, tiled=True)]
    unnamed x18 -> x6, local copies, waits for them, and re-layouts: 10.7 us -> 0.01 us
    all_to_all x1 -> x0, starting transfers between devices: 6.27 us -> none  [on_device(): got = lax.all_to_all(sent, VOX, 0, 0, tiled=True)]
    ppermute x3 -> x1, starting transfers between devices: 8.42 us -> 4.21 us  [on_device(): other = lax.ppermute(grad, 'z_hi', [(0, 1), (1, 0)])]
    ppermute x3 -> x1, waiting for transfers between devices: 5.54 us -> 1.84 us  [on_device(): other = lax.ppermute(grad, 'z_hi', [(0, 1), (1, 0)])]
    pallas_call x1, Pallas kernels: 4.11 us -> 6.82 us  [on_device(): pl.pallas_call(forward_kernel, out_shape=(jax.ShapeDtypeStruct((OWNERS, R...]
    all_to_all x1 -> x0, waiting for transfers between devices: 2.63 us -> none  [on_device(): got = lax.all_to_all(sent, VOX, 0, 0, tiled=True)]
    pallas_call x1 -> x2, Pallas kernels: 4.62 us -> 3.66 us  [the longest x1 3.36 us: on_device(): pl.pallas_call(backward_kernel, out_shape=jax.ShapeDtypeStruct((1, 2, 512...]
  transfers between devices with their start and end apart: 5 -> 2, of which waited for: 4 -> 2; matrix products, arithmetic and copies ran while one was open for 0% -> 0% of each run, Pallas kernels for 0% -> 0%
where the time goes in v2:
time: 64.2 us; the launch traced here: 64 us
  blocking collectives  39.6 us (62%)
  Pallas kernels  12.1 us (19%)
  starting transfers between devices  7.73 us (12%)
  waiting for transfers between devices  2.67 us (4%)
  between operations  1.34 us (2%)
    all_to_all x2, blocking collectives, on_device(): got = lax.all_to_all(sent, VOX, 0, 0, tiled=True)  39.6 us
    pallas_call x1, Pallas kernels, on_device(): pl.pallas_call(forward_kernel, out_shape=(jax.ShapeDtypeStruct((OWNERS, R...  6.82 us
    ppermute x1, starting transfers between devices, on_device(): other = lax.ppermute(grad, 'z_hi', [(0, 1), (1, 0)])  4.21 us
    ppermute x1, starting transfers between devices, on_device(): grad = grad + lax.ppermute(grad, 'core', [(0, 1), (1, 0)])  3.52 us
    pallas_call x1, Pallas kernels, on_device(): pl.pallas_call(backward_kernel, out_shape=jax.ShapeDtypeStruct((1, 2, 512...  3.36 us
    ppermute x1, waiting for transfers between devices, on_device(): other = lax.ppermute(grad, 'z_hi', [(0, 1), (1, 0)])  1.84 us
    pallas_call x1, Pallas kernels, on_device(): pl.pallas_call(owner_kernel, out_shape=(jax.ShapeDtypeStruct((OWNERS, ROW...  1.58 us
  transfers between devices with their start and end apart: 2, of which 2 were waited for; matrix products, arithmetic and copies ran while one was open for 0% of the time, Pallas kernels for 0%

profile of v2, /device:TPU:1, one launch (start us, length us, event | category | flops | bytes accessed | tf_op | source)
XLA Modules:
  0.0 64.0 jit_solution(5846489493554585132)
XLA Ops:
  0.6 0.0 copy-start.2
  0.6 0.0 copy-start.1
  1.3 0.0 copy-start
  1.3 6.8 %forward.1 = (bf16[64,16,128]{2,1,0:T(8,128)(2,1)S(1)}, f32[64,128]{1,0:T(8,128)S(1)}, bf16[5,1024,1024]{2,1,0:T(8,128)(2,1)S(1)}) custom-call(s32[1,1,5]{2,1,0:T(1,128)} %ids.1, s32[1,1,5]{2,1,0:T(1,128)} %starts.1, s32[1,1]{1,0:T(1,128)S(6)} %copy.8.counts, f32[1,2,512]{2,1,0:T(2,128)} %image.1, bf16[1,1,5,1024,1024]{4,3,2,1,0:T(8,128)(2,1)} %weights.1, ...), custom_call_target="tpu_custom_call" | custom-call | tf_op jit(solution)/shard_map/forward/pallas_call | solution.py:338
  8.2 23.3 %all_to_all.10.got = bf16[64,16,128]{2,1,0:T(8,128)(2,1)S(1)} all-to-all(bf16[64,16,128]{2,1,0:T(8,128)(2,1)S(1)} %get-tuple-element.7), channel_id=1, replica_groups=mesh['y'=4,'x'=4,'z_lo'=4,'z_hi'=2,'core'=2] {'y','x','z_lo'}, dimensions={0} | all-to-all | bytes 524288 | tf_op jit(solution)/shard_map/all_to_all | solution.py:367
  31.5 1.6 %owner.1 = (bf16[64,16,128]{2,1,0:T(8,128)(2,1)S(1)}, f32[1,4,2048]{2,1,0:T(4,128)}) custom-call(bf16[64,16,128]{2,1,0:T(8,128)(2,1)S(1)} %all_to_all.10.got, f32[64,128]{1,0:T(8,128)S(1)} %get-tuple-element.8.spread), custom_call_target="tpu_custom_call" | custom-call | tf_op jit(solution)/shard_map/owner/pallas_call | solution.py:368
  33.0 16.3 %all_to_all.11.got = bf16[64,16,128]{2,1,0:T(8,128)(2,1)S(1)} all-to-all(bf16[64,16,128]{2,1,0:T(8,128)(2,1)S(1)} %get-tuple-element.9), channel_id=1, replica_groups=mesh['y'=4,'x'=4,'z_lo'=4,'z_hi'=2,'core'=2] {'y','x','z_lo'}, dimensions={0} | all-to-all | bytes 524288 | tf_op jit(solution)/shard_map/all_to_all | solution.py:380
  49.4 0.0 copy-done.2
  49.4 0.0 copy-done.1
  49.4 3.4 %backward.1 = f32[1,2,512]{2,1,0:T(2,128)S(1)} custom-call(s32[1,1,5]{2,1,0:T(1,128)S(1)} %copy-done.1, s32[1,1,5]{2,1,0:T(1,128)S(1)} %copy-done.2, s32[1,1]{1,0:T(1,128)S(6)} %copy.8.counts, bf16[64,16,128]{2,1,0:T(8,128)(2,1)S(1)} %all_to_all.11.got, bf16[5,1024,1024]{2,1,0:T(8,128)(2,1)S(1)} %get-tuple-element.10.held), custom_call_target="tpu_custom_call" | custom-call | tf_op jit(solution)/shard_map/backward/pallas_call | solution.py:381
  52.7 3.5 %collective-permute-start = (f32[1,2,512]{2,1,0:T(2,128)S(1)}, f32[1,2,512]{2,1,0:T(2,128)S(1)}, u32[]{:S(2)}, u32[]{:S(2)}) collective-permute-start(f32[1,2,512]{2,1,0:T(2,128)S(1)} %backward.1), channel_id=1, source_target_pairs={{0,1},{1,0},{2,3},{3,2},{4,5},{5,4},{6,7},{7,6},{8,9},{9,8},{10,11... | collective-permute-start | bytes 12296 | tf_op jit(solution)/shard_map/ppermute | solution.py:390
  56.2 0.8 %collective-permute-done = f32[1,2,512]{2,1,0:T(2,128)S(1)} collective-permute-done((f32[1,2,512]{2,1,0:T(2,128)S(1)}, f32[1,2,512]{2,1,0:T(2,128)S(1)}, u32[]{:S(2)}, u32[]{:S(2)}) %collective-permute-start) | collective-permute-done | bytes 4128 | tf_op jit(solution)/shard_map/ppermute | solution.py:390
  57.1 4.2 %collective-permute-start.1 = (f32[1,2,512]{2,1,0:T(2,128)S(1)}, f32[1,2,512]{2,1,0:T(2,128)S(1)}, u32[]{:S(2)}, u32[]{:S(2)}) collective-permute-start(f32[1,2,512]{2,1,0:T(2,128)S(1)} %add.6), channel_id=1, source_target_pairs={{0,2},{2,0},{1,3},{3,1},{4,6},{6,4},{5,7},{7,5},{8,10},{10,8},{9,1... | collective-permute-start | bytes 12296 | tf_op jit(solution)/shard_map/ppermute | solution.py:391
  61.3 0.0 copy-done
  61.3 0.3 smooth.1
  61.6 1.8 %collective-permute-done.1 = f32[1,2,512]{2,1,0:T(2,128)S(1)} collective-permute-done((f32[1,2,512]{2,1,0:T(2,128)S(1)}, f32[1,2,512]{2,1,0:T(2,128)S(1)}, u32[]{:S(2)}, u32[]{:S(2)}) %collective-permute-start.1) | collective-permute-done | bytes 4128 | tf_op jit(solution)/shard_map/ppermute | solution.py:391
  63.4 0.6 multiply_subtract_fusion
  (1 shorter events, 0.0 us)
Async XLA Ops:
  0.6 48.7 %copy-start.2 = (s32[1,1,5]{2,1,0:T(1,128)S(1)}, s32[1,1,5]{2,1,0:T(1,128)}, u32[]{:S(2)}) copy-start(s32[1,1,5]{2,1,0:T(1,128)} %starts.1) | copy-start | bytes 64
  0.6 48.7 %copy-start.1 = (s32[1,1,5]{2,1,0:T(1,128)S(1)}, s32[1,1,5]{2,1,0:T(1,128)}, u32[]{:S(2)}) copy-start(s32[1,1,5]{2,1,0:T(1,128)} %ids.1) | copy-start | bytes 64
  1.3 60.0 %copy-start = (f32[1,2,512]{2,1,0:T(2,128)S(1)}, f32[1,2,512]{2,1,0:T(2,128)}, u32[]{:S(2)}) copy-start(f32[1,2,512]{2,1,0:T(2,128)} %image.1) | copy-start | bytes 12292
  52.7 4.3 %collective-permute-start = (f32[1,2,512]{2,1,0:T(2,128)S(1)}, f32[1,2,512]{2,1,0:T(2,128)S(1)}, u32[]{:S(2)}, u32[]{:S(2)}) collective-permute-start(f32[1,2,512]{2,1,0:T(2,128)S(1)} %backward.1), channel_id=1, source_target_pairs={{0,1},{1,0},{2,3},{3,2},{4,5},{5,4},{6,7},{7,6},{8,9},{9,8},{10,11... | collective-permute-start | bytes 12296 | tf_op jit(solution)/shard_map/ppermute | solution.py:390
  57.1 6.4 %collective-permute-start.1 = (f32[1,2,512]{2,1,0:T(2,128)S(1)}, f32[1,2,512]{2,1,0:T(2,128)S(1)}, u32[]{:S(2)}, u32[]{:S(2)}) collective-permute-start(f32[1,2,512]{2,1,0:T(2,128)S(1)} %add.6), channel_id=1, source_target_pairs={{0,2},{2,0},{1,3},{3,1},{4,6},{6,4},{5,7},{7,5},{8,10},{10,8},{9,1... | collective-permute-start | bytes 12296 | tf_op jit(solution)/shard_map/ppermute | solution.py:391

commit v3 on v2

--- a/solution.py
+++ b/solution.py
@@ -16,7 +16,8 @@
 LANES = 128
 ROWS = 16
 OWNERS = 64
-CHUNKS = 2
+ON_MATRIX = 2
+IN_FLIGHT = 3
 STEP_SIZE = 0.25
 TV_WEIGHT = 0.3
 TV_EPS = 0.01
@@ -75,15 +76,11 @@
     ):
         small.append(pltpu.make_async_copy(src, dst, small_sems.at[i]))
         small[-1].start()
-    depth = VOXELS // CHUNKS
-    copies = {}
-    for k in range(K_MAX):
-        for c in range(CHUNKS):
-            span = pl.ds(c * depth, depth)
-            copies[k, c] = pltpu.make_async_copy(
-                weights.at[0, 0, k, span], held.at[k, span], sems.at[k * CHUNKS + c]
-            )
-            copies[k, c].start()
+    copies = [
+        pltpu.make_async_copy(weights.at[0, 0, k], held.at[k], sems.at[k]) for k in range(K_MAX)
+    ]
+    for copy in copies[:IN_FLIGHT]:
+        copy.start()
     for copy in small:
         copy.wait()
 
@@ -114,15 +111,16 @@
         code_tile = jnp.where(here & (lane < WIN), code.astype(jnp.float32), code_tile)
         block_tile = jnp.where(here & (lane < WIN), block, block_tile)
 
-    for k in range(K_MAX):
-        piece = jnp.zeros((1, CELLS), jnp.float32)
-        for c in range(CHUNKS):
-            copies[k, c].wait()
-            piece = piece + jnp.dot(
-                voxels[:, c * depth : (c + 1) * depth],
-                held[k, c * depth : (c + 1) * depth, :],
-                preferred_element_type=jnp.float32,
-            )
+    for d in range(OWNERS):
+        own_halo = jnp.broadcast_to(halo[d : d + 1, :], (8, LANES))
+        marked = jnp.where(block_tile == d // 4, code_tile, base)
+        sent[d, 8:16, :] = jnp.where(row == 7, own_halo, marked).astype(jnp.bfloat16)
+
+    for k in range(K_MAX):
+        copies[k].wait()
+        if k + IN_FLIGHT < K_MAX:
+            copies[k + IN_FLIGHT].start()
+        piece = jnp.dot(voxels, held[k], preferred_element_type=jnp.float32)
         tile = jnp.concatenate([piece[:, i * LANES : (i + 1) * LANES] for i in range(8)], axis=0)
         low = lax.rem(starts[0, 0, k], WIN)
         tile = jnp.where(
@@ -136,12 +134,10 @@
                 for b in range(16):
                     sent[4 * b + q, 0:8, :] = data
 
+    last = [tiles[q, 8:10, :].astype(jnp.bfloat16) for q in range(4)]
     for q in range(4):
-        full = jnp.where(row < 2, tiles[q, 8:16, :], base)
         for b in range(16):
-            own_halo = jnp.broadcast_to(halo[4 * b + q : 4 * b + q + 1, :], (8, LANES))
-            marked = jnp.where(block_tile == b, code_tile, full)
-            sent[4 * b + q, 8:16, :] = jnp.where(row == 7, own_halo, marked).astype(jnp.bfloat16)
+            sent[4 * b + q, 8:10, :] = last[q]
 
 
 def derivative(x):
@@ -286,36 +282,46 @@
 
 
 def backward_kernel(ids, starts, counts, got, held, grad, wins):
-    depth = VOXELS // 2
     live = counts[0, 0]
     lane = lane_iota((8, LANES))
-    vectors = []
     for k in range(K_MAX):
         block = ids[0, 0, k]
         for q in range(4):
             strip = got[4 * block + q].astype(jnp.float32)
-            wins[2 * q : 2 * q + 2, :] = strip[2 * k : 2 * k + 2, :]
+            wins[k, 2 * q : 2 * q + 2, :] = strip[2 * k : 2 * k + 2, :]
+    windows = []
+    for k in range(K_MAX):
         low = lax.rem(starts[0, 0, k], WIN)
-        tile = wins[...]
+        tile = wins[k]
         tile = jnp.where(
             (lane & (WIN - 1)) < WIN - low,
             pltpu.roll(tile, lax.rem(LANES - low, LANES), 1),
             pltpu.roll(tile, WIN - low, 1),
         )
-        tile = jnp.where(k < live, tile, 0.0)
-        vectors.append(
-            jnp.concatenate([tile[i : i + 1, :] for i in range(8)], axis=1).astype(jnp.bfloat16)
-        )
-    for c in range(2):
-        total = jnp.zeros((1, depth), jnp.float32)
-        for k in range(K_MAX):
+        windows.append(jnp.where(k < live, tile, 0.0))
+    vectors = [
+        jnp.concatenate([windows[k][i : i + 1, :] for i in range(8)], axis=1).astype(jnp.bfloat16)
+        for k in range(ON_MATRIX)
+    ]
+    for j in range(8):
+        rows = slice(j * LANES, (j + 1) * LANES)
+        total = jnp.zeros((1, LANES), jnp.float32)
+        for k in range(ON_MATRIX):
             total = total + lax.dot_general(
                 vectors[k],
-                held[k, c * depth : (c + 1) * depth, :],
+                held[k, rows, :],
                 (((1,), (1,)), ((), ())),
                 preferred_element_type=jnp.float32,
             )
-        grad[0, c : c + 1, :] = total
+        partial = jnp.zeros((LANES, LANES), jnp.float32)
+        for k in range(ON_MATRIX, K_MAX):
+            block = held[k, rows, :].astype(jnp.float32)
+            for i in range(8):
+                weight = jnp.broadcast_to(windows[k][i : i + 1, :], (LANES, LANES))
+                partial = partial + block[:, i * LANES : (i + 1) * LANES] * weight
+        total = total + jnp.sum(partial.T, axis=0, keepdims=True)
+        y, t = j // 4, j % 4
+        grad[0, y : y + 1, t * LANES : (t + 1) * LANES] = total
 
 
 def smem():
@@ -352,7 +358,7 @@
             pltpu.VMEM((4, ROWS, LANES), jnp.float32),
             pltpu.VMEM((OWNERS, LANES), jnp.float32),
             pltpu.SemaphoreType.DMA((4,)),
-            pltpu.SemaphoreType.DMA((K_MAX * CHUNKS,)),
+            pltpu.SemaphoreType.DMA((K_MAX,)),
         ],
         compiler_params=pltpu.CompilerParams(vmem_limit_bytes=20 * MIB),
         name="forward",
@@ -383,7 +389,7 @@
         out_shape=jax.ShapeDtypeStruct((1, 2, 512), jnp.float32),
         in_specs=[smem(), smem(), smem(), vmem(), vmem()],
         out_specs=vmem(),
-        scratch_shapes=[pltpu.VMEM((8, LANES), jnp.float32)],
+        scratch_shapes=[pltpu.VMEM((K_MAX, 8, LANES), jnp.float32)],
         compiler_params=pltpu.CompilerParams(vmem_limit_bytes=20 * MIB),
         name="backward",
     )(block_ids, offsets, counts, got, held)

time: 64.2 us -> 61.5 us (0.958)
  Pallas kernels: 12.1 us -> 9.33 us
    pallas_call x1, Pallas kernels: 6.82 us -> 5.11 us  [on_device(): pl.pallas_call(forward_kernel, out_shape=(jax.ShapeDtypeStruct((OWNERS, R...]
    pallas_call x1, Pallas kernels: 3.36 us -> 2.35 us  [on_device(): pl.pallas_call(backward_kernel, out_shape=jax.ShapeDtypeStruct((1, 2, 512...]
where the time goes in v3:
time: 61.5 us; the launch traced here: 61.4 us
  blocking collectives  39.6 us (64%)
  Pallas kernels  9.33 us (15%)
  starting transfers between devices  7.77 us (13%)
  waiting for transfers between devices  2.66 us (4%)
  between operations  1.34 us (2%)
    all_to_all x2, blocking collectives, on_device(): got = lax.all_to_all(sent, VOX, 0, 0, tiled=True)  39.6 us
    pallas_call x1, Pallas kernels, on_device(): pl.pallas_call(forward_kernel, out_shape=(jax.ShapeDtypeStruct((OWNERS, R...  5.11 us
    ppermute x1, starting transfers between devices, on_device(): other = lax.ppermute(grad, 'z_hi', [(0, 1), (1, 0)])  4.21 us
    ppermute x1, starting transfers between devices, on_device(): grad = grad + lax.ppermute(grad, 'core', [(0, 1), (1, 0)])  3.55 us
    pallas_call x1, Pallas kernels, on_device(): pl.pallas_call(backward_kernel, out_shape=jax.ShapeDtypeStruct((1, 2, 512...  2.35 us
    ppermute x1, waiting for transfers between devices, on_device(): other = lax.ppermute(grad, 'z_hi', [(0, 1), (1, 0)])  1.84 us
    pallas_call x1, Pallas kernels, on_device(): pl.pallas_call(owner_kernel, out_shape=(jax.ShapeDtypeStruct((OWNERS, ROW...  1.57 us
  transfers between devices with their start and end apart: 2, of which 2 were waited for; matrix products, arithmetic and copies ran while one was open for 0% of the time, Pallas kernels for 0%

profile of v3, /device:TPU:1, one launch (start us, length us, event | category | flops | bytes accessed | tf_op | source)
XLA Modules:
  0.0 61.4 jit_solution(16428202651891972276)
XLA Ops:
  0.6 0.0 copy-start.2
  0.6 0.0 copy-start.1
  1.3 0.0 copy-start
  1.3 5.1 %forward.1 = (bf16[64,16,128]{2,1,0:T(8,128)(2,1)S(1)}, f32[64,128]{1,0:T(8,128)S(1)}, bf16[5,1024,1024]{2,1,0:T(8,128)(2,1)S(1)}) custom-call(s32[1,1,5]{2,1,0:T(1,128)} %ids.1, s32[1,1,5]{2,1,0:T(1,128)} %starts.1, s32[1,1]{1,0:T(1,128)S(6)} %copy.8.counts, f32[1,2,512]{2,1,0:T(2,128)} %image.1, bf16[1,1,5,1024,1024]{4,3,2,1,0:T(8,128)(2,1)} %weights.1, ...), custom_call_target="tpu_custom_call" | custom-call | tf_op jit(solution)/shard_map/forward/pallas_call | solution.py:344
  6.4 23.3 %all_to_all.10.got = bf16[64,16,128]{2,1,0:T(8,128)(2,1)S(1)} all-to-all(bf16[64,16,128]{2,1,0:T(8,128)(2,1)S(1)} %get-tuple-element.7), channel_id=1, replica_groups=mesh['y'=4,'x'=4,'z_lo'=4,'z_hi'=2,'core'=2] {'y','x','z_lo'}, dimensions={0} | all-to-all | bytes 524288 | tf_op jit(solution)/shard_map/all_to_all | solution.py:373
  29.8 1.6 %owner.1 = (bf16[64,16,128]{2,1,0:T(8,128)(2,1)S(1)}, f32[1,4,2048]{2,1,0:T(4,128)}) custom-call(bf16[64,16,128]{2,1,0:T(8,128)(2,1)S(1)} %all_to_all.10.got, f32[64,128]{1,0:T(8,128)S(1)} %get-tuple-element.8.spread), custom_call_target="tpu_custom_call" | custom-call | tf_op jit(solution)/shard_map/owner/pallas_call | solution.py:374
  31.3 16.3 %all_to_all.11.got = bf16[64,16,128]{2,1,0:T(8,128)(2,1)S(1)} all-to-all(bf16[64,16,128]{2,1,0:T(8,128)(2,1)S(1)} %get-tuple-element.9), channel_id=1, replica_groups=mesh['y'=4,'x'=4,'z_lo'=4,'z_hi'=2,'core'=2] {'y','x','z_lo'}, dimensions={0} | all-to-all | bytes 524288 | tf_op jit(solution)/shard_map/all_to_all | solution.py:386
  47.7 0.0 copy-done.2
  47.7 0.0 copy-done.1
  47.7 2.3 %backward.1 = f32[1,2,512]{2,1,0:T(2,128)S(1)} custom-call(s32[1,1,5]{2,1,0:T(1,128)S(1)} %copy-done.1, s32[1,1,5]{2,1,0:T(1,128)S(1)} %copy-done.2, s32[1,1]{1,0:T(1,128)S(6)} %copy.8.counts, bf16[64,16,128]{2,1,0:T(8,128)(2,1)S(1)} %all_to_all.11.got, bf16[5,1024,1024]{2,1,0:T(8,128)(2,1)S(1)} %get-tuple-element.10.held), custom_call_target="tpu_custom_call" | custom-call | tf_op jit(solution)/shard_map/backward/pallas_call | solution.py:387
  50.0 3.6 %collective-permute-start = (f32[1,2,512]{2,1,0:T(2,128)S(1)}, f32[1,2,512]{2,1,0:T(2,128)S(1)}, u32[]{:S(2)}, u32[]{:S(2)}) collective-permute-start(f32[1,2,512]{2,1,0:T(2,128)S(1)} %backward.1), channel_id=1, source_target_pairs={{0,1},{1,0},{2,3},{3,2},{4,5},{5,4},{6,7},{7,6},{8,9},{9,8},{10,11... | collective-permute-start | bytes 12296 | tf_op jit(solution)/shard_map/ppermute | solution.py:396
  53.6 0.8 %collective-permute-done = f32[1,2,512]{2,1,0:T(2,128)S(1)} collective-permute-done((f32[1,2,512]{2,1,0:T(2,128)S(1)}, f32[1,2,512]{2,1,0:T(2,128)S(1)}, u32[]{:S(2)}, u32[]{:S(2)}) %collective-permute-start) | collective-permute-done | bytes 4128 | tf_op jit(solution)/shard_map/ppermute | solution.py:396
  54.4 4.2 %collective-permute-start.1 = (f32[1,2,512]{2,1,0:T(2,128)S(1)}, f32[1,2,512]{2,1,0:T(2,128)S(1)}, u32[]{:S(2)}, u32[]{:S(2)}) collective-permute-start(f32[1,2,512]{2,1,0:T(2,128)S(1)} %add.6), channel_id=1, source_target_pairs={{0,2},{2,0},{1,3},{3,1},{4,6},{6,4},{5,7},{7,5},{8,10},{10,8},{9,1... | collective-permute-start | bytes 12296 | tf_op jit(solution)/shard_map/ppermute | solution.py:397
  58.6 0.0 copy-done
  58.6 0.3 smooth.1
  58.9 1.8 %collective-permute-done.1 = f32[1,2,512]{2,1,0:T(2,128)S(1)} collective-permute-done((f32[1,2,512]{2,1,0:T(2,128)S(1)}, f32[1,2,512]{2,1,0:T(2,128)S(1)}, u32[]{:S(2)}, u32[]{:S(2)}) %collective-permute-start.1) | collective-permute-done | bytes 4128 | tf_op jit(solution)/shard_map/ppermute | solution.py:397
  60.8 0.6 multiply_subtract_fusion
  (1 shorter events, 0.0 us)
Async XLA Ops:
  0.6 47.0 %copy-start.2 = (s32[1,1,5]{2,1,0:T(1,128)S(1)}, s32[1,1,5]{2,1,0:T(1,128)}, u32[]{:S(2)}) copy-start(s32[1,1,5]{2,1,0:T(1,128)} %starts.1) | copy-start | bytes 64
  0.6 47.0 %copy-start.1 = (s32[1,1,5]{2,1,0:T(1,128)S(1)}, s32[1,1,5]{2,1,0:T(1,128)}, u32[]{:S(2)}) copy-start(s32[1,1,5]{2,1,0:T(1,128)} %ids.1) | copy-start | bytes 64
  1.3 57.3 %copy-start = (f32[1,2,512]{2,1,0:T(2,128)S(1)}, f32[1,2,512]{2,1,0:T(2,128)}, u32[]{:S(2)}) copy-start(f32[1,2,512]{2,1,0:T(2,128)} %image.1) | copy-start | bytes 12292
  50.0 4.4 %collective-permute-start = (f32[1,2,512]{2,1,0:T(2,128)S(1)}, f32[1,2,512]{2,1,0:T(2,128)S(1)}, u32[]{:S(2)}, u32[]{:S(2)}) collective-permute-start(f32[1,2,512]{2,1,0:T(2,128)S(1)} %backward.1), channel_id=1, source_target_pairs={{0,1},{1,0},{2,3},{3,2},{4,5},{5,4},{6,7},{7,6},{8,9},{9,8},{10,11... | collective-permute-start | bytes 12296 | tf_op jit(solution)/shard_map/ppermute | solution.py:396
  54.4 6.4 %collective-permute-start.1 = (f32[1,2,512]{2,1,0:T(2,128)S(1)}, f32[1,2,512]{2,1,0:T(2,128)S(1)}, u32[]{:S(2)}, u32[]{:S(2)}) collective-permute-start(f32[1,2,512]{2,1,0:T(2,128)S(1)} %add.6), channel_id=1, source_target_pairs={{0,2},{2,0},{1,3},{3,1},{4,6},{6,4},{5,7},{7,5},{8,10},{10,8},{9,1... | collective-permute-start | bytes 12296 | tf_op jit(solution)/shard_map/ppermute | solution.py:397

commit v4 on v3

--- a/solution.py
+++ b/solution.py
@@ -14,7 +14,8 @@
 VOXELS = 1024
 CELLS = SB * WIN
 LANES = 128
-ROWS = 16
+TILES = K_MAX + 1
+WIDTH = TILES * LANES
 OWNERS = 64
 ON_MATRIX = 2
 IN_FLIGHT = 3
@@ -60,7 +61,6 @@
     starts,
     image,
     measured,
-    tiles,
     halo,
     small_sems,
     sems,
@@ -91,14 +91,13 @@
 
     plane = as_tile(image)
     turned = jnp.concatenate(split_three(plane) + [jnp.zeros((104, LANES), jnp.float32)], axis=0).T
-    halo[...] = turned[0:64] + pltpu.roll(turned[64:128], 24, 1)
+    halo[...] = pltpu.roll(turned, 32, 1)
 
     voxels = jnp.concatenate([image[0, 0:1, :], image[0, 1:2, :]], axis=1).astype(jnp.bfloat16)
-    lane = lane_iota((8, LANES))
-    row = lax.broadcasted_iota(jnp.int32, (8, LANES), 0)
-    base = jnp.full((8, LANES), NOWHERE, jnp.float32)
-    code_tile = jnp.full((8, LANES), NOWHERE, jnp.float32)
-    block_tile = jnp.full((8, LANES), -1, jnp.int32)
+    lane2 = lane_iota((2, LANES))
+    base = jnp.full((2, LANES), NOWHERE, jnp.float32)
+    code_row = base
+    block_row = jnp.full((2, LANES), -1, jnp.int32)
     live = counts[0, 0]
     for k in range(K_MAX):
         start = starts[0, 0, k]
@@ -106,16 +105,18 @@
         low = start - coarse * WIN
         code = (coarse & 1) * 16 + (coarse >> 1)
         block = jnp.where(k < live, ids[0, 0, k], -1)
-        here = row == 2 + k
-        base = jnp.where(here & (lane >= WIN), low.astype(jnp.float32), base)
-        code_tile = jnp.where(here & (lane < WIN), code.astype(jnp.float32), code_tile)
-        block_tile = jnp.where(here & (lane < WIN), block, block_tile)
-
-    for d in range(OWNERS):
-        own_halo = jnp.broadcast_to(halo[d : d + 1, :], (8, LANES))
-        marked = jnp.where(block_tile == d // 4, code_tile, base)
-        sent[d, 8:16, :] = jnp.where(row == 7, own_halo, marked).astype(jnp.bfloat16)
-
+        base = jnp.where(lane2 == 8 + k, low.astype(jnp.float32), base)
+        code_row = jnp.where(lane2 == k, code.astype(jnp.float32), code_row)
+        block_row = jnp.where(lane2 == k, block, block_row)
+    for b in range(16):
+        marked = jnp.where(block_row == b, code_row, base)
+        for d in range(4 * b, 4 * b + 4):
+            own_halo = halo[pl.ds(d, 2, stride=OWNERS), :]
+            sent[d, :, K_MAX * LANES :] = jnp.where(lane2 < 32, marked, own_halo).astype(
+                jnp.bfloat16
+            )
+
+    lane = lane_iota((8, LANES))
     for k in range(K_MAX):
         copies[k].wait()
         if k + IN_FLIGHT < K_MAX:
@@ -127,17 +128,9 @@
             (lane & (WIN - 1)) >= low, pltpu.roll(tile, low, 1), pltpu.roll(tile, low + WIN, 1)
         )
         for q in range(4):
-            tiles[q, 2 * k : 2 * k + 2, :] = tile[2 * q : 2 * q + 2, :]
-        if k == 3:
-            for q in range(4):
-                data = tiles[q, 0:8, :].astype(jnp.bfloat16)
-                for b in range(16):
-                    sent[4 * b + q, 0:8, :] = data
-
-    last = [tiles[q, 8:10, :].astype(jnp.bfloat16) for q in range(4)]
-    for q in range(4):
-        for b in range(16):
-            sent[4 * b + q, 8:10, :] = last[q]
+            strip = tile[2 * q : 2 * q + 2, :].astype(jnp.bfloat16)
+            for b in range(16):
+                sent[4 * b + q, :, k * LANES : (k + 1) * LANES] = strip
 
 
 def derivative(x):
@@ -158,84 +151,72 @@
 
 
 def owner_kernel(got, spread, sent, residual, wide):
-    wide[...] = got[...].astype(jnp.float32).reshape(OWNERS * ROWS, LANES)
-    lane = lane_iota((OWNERS, LANES))
-    low_half = lane < WIN
+    for d in range(OWNERS):
+        wide[2 * d : 2 * d + 2, :] = got[d].astype(jnp.float32)
+    lane = lane_iota((LANES, LANES))
+    parity = lax.broadcasted_iota(jnp.int32, (LANES, LANES), 0) & 1
     within = (lane & (WIN - 1)).astype(jnp.float32)
-    slot = jnp.where(low_half, lane & 31, 0).astype(jnp.float32)
+    own_half = (lane >> 6) == parity
+    first_half = (lane & 32) == 0
+    slot = jnp.where(own_half, lane & 31, -1).astype(jnp.float32)
+    info = wide[:, K_MAX * LANES :]
     places, strips, later = [], [], []
     for k in range(K_MAX):
-        info = wide[pl.ds(10 + k, OWNERS, stride=ROWS), :]
-        turned = pltpu.roll(info, WIN, 1)
-        code = jnp.where(low_half, info, turned)
-        low = jnp.where(low_half, turned, info)
+        code = jnp.broadcast_to(info[:, k : k + 1], (LANES, LANES))
+        low = jnp.broadcast_to(info[:, 8 + k : 9 + k], (LANES, LANES))
         following = jnp.where(code >= 16.0, code - 15.0, code + 16.0)
-        wanted = jnp.where(lane < 32, code, following)
-        places.append(jnp.where(low_half & (wanted == slot), 1.0, 0.0))
+        wanted = jnp.where(first_half, code, following)
+        places.append(jnp.where(wanted == slot, 1.0, 0.0))
         first = within >= low
         later.append(first)
-        parts = []
-        for u in range(2):
-            strip = wide[pl.ds(2 * k + u, OWNERS, stride=ROWS), :]
-            parts.append((jnp.where(first, strip, 0.0), jnp.where(first, 0.0, strip)))
+        strip = wide[:, k * LANES : (k + 1) * LANES]
         strips.append(
-            jnp.concatenate([parts[0][0], parts[1][0], parts[0][1], parts[1][1]], axis=1)
+            jnp.concatenate([jnp.where(first, strip, 0.0), jnp.where(first, 0.0, strip)], axis=1)
         )
     place = jnp.concatenate(places, axis=0).astype(jnp.bfloat16)
     strip = jnp.concatenate(strips, axis=0).astype(jnp.bfloat16)
     both = lax.dot_general(
         place, strip, (((0,), (0,)), ((), ())), preferred_element_type=jnp.float32
     )
-    summed = both[0:32, 0:256] + both[32:64, 256:512]
     lane16 = lane_iota((16, LANES)) < WIN
     rows = []
     for u in range(2):
-        even = summed[0:16, u * LANES : (u + 1) * LANES]
-        odd = summed[16:32, u * LANES : (u + 1) * LANES]
+        summed = both[64 * u : 64 * u + 32, :LANES] + both[64 * u + 32 : 64 * u + 64, LANES:]
+        even = summed[0:16]
+        odd = summed[16:32]
         rows.append(jnp.where(lane16, even, pltpu.roll(odd, WIN, 1)))
         rows.append(jnp.where(lane16, pltpu.roll(even, WIN, 1), odd))
     signals = jnp.concatenate(rows, axis=0)
     resid = derivative(signals) - spread[...]
     adjoint = -derivative(resid)
-    packed = []
+    zero = jnp.zeros((32, LANES), jnp.float32)
+    table = []
     for u in range(2):
         a = adjoint[32 * u : 32 * u + 16]
         b = adjoint[32 * u + 16 : 32 * u + 32]
-        packed.append(
-            (
+        half = jnp.concatenate(
+            [
                 jnp.where(lane16, a, pltpu.roll(b, WIN, 1)),
                 jnp.where(lane16, pltpu.roll(a, WIN, 1), b),
-            )
-        )
-    table = jnp.concatenate(
-        [jnp.concatenate([packed[0][p], packed[1][p]], axis=1) for p in range(2)], axis=0
+            ],
+            axis=0,
+        )
+        table.append(jnp.concatenate([half, zero], axis=1))
+        table.append(jnp.concatenate([zero, half], axis=1))
+    table = jnp.concatenate(table, axis=0).astype(jnp.bfloat16)
+    cut = jnp.dot(place, table, preferred_element_type=jnp.float32)
+    for k in range(K_MAX):
+        mine = cut[k * LANES : (k + 1) * LANES]
+        wide[:, k * LANES : (k + 1) * LANES] = jnp.where(
+            later[k], mine[:, :LANES], mine[:, LANES:]
+        )
+    wide[:, K_MAX * LANES :] = jnp.where(
+        lane < WIN,
+        pltpu.roll(info, 2, 0),
+        pltpu.roll(pltpu.roll(info, LANES - 2, 0), 32, 1),
     )
-    zero = jnp.zeros_like(table)
-    table = jnp.concatenate(
-        [
-            jnp.concatenate([table, zero], axis=1),
-            jnp.concatenate([zero, table], axis=1),
-            jnp.zeros((64, 512), jnp.float32),
-        ],
-        axis=0,
-    ).astype(jnp.bfloat16)
-    cut = jnp.dot(place, table, preferred_element_type=jnp.float32)
-    for k in range(K_MAX):
-        mine = cut[k * OWNERS : (k + 1) * OWNERS]
-        for u in range(2):
-            window = jnp.where(
-                later[k],
-                mine[:, u * LANES : (u + 1) * LANES],
-                mine[:, 256 + u * LANES : 256 + (u + 1) * LANES],
-            )
-            wide[pl.ds(2 * k + u, OWNERS, stride=ROWS), :] = window
-    shard = wide[pl.ds(15, OWNERS, stride=ROWS), :]
-    wide[pl.ds(10, OWNERS, stride=ROWS), :] = jnp.where(
-        low_half,
-        pltpu.roll(shard, 1, 0),
-        pltpu.roll(pltpu.roll(shard, OWNERS - 1, 0), WIN, 1),
-    )
-    sent[...] = wide[...].reshape(OWNERS, ROWS, LANES).astype(jnp.bfloat16)
+    for d in range(OWNERS):
+        sent[d] = wide[2 * d : 2 * d + 2, :].astype(jnp.bfloat16)
     for r in range(4):
         for h in range(16):
             residual[0, r : r + 1, h * LANES : (h + 1) * LANES] = resid[
@@ -269,12 +250,13 @@
 
 def smooth_kernel(got, image, base, wide):
     vox = lax.axis_index(VOX)
-    wide[...] = got[:, 8:16, :].astype(jnp.float32).reshape(OWNERS * 8, LANES)
-    shard = wide[pl.ds(2, OWNERS, stride=8), :]
+    for d in range(OWNERS):
+        wide[2 * d : 2 * d + 2, :] = got[d, :, K_MAX * LANES :].astype(jnp.float32)
+    shard = jnp.concatenate([wide[pl.ds(u, OWNERS, stride=2), :] for u in range(2)], axis=0)
     whole = shard + (pltpu.roll(shard, LANES - 8, 1) + pltpu.roll(shard, LANES - 16, 1))
-    turned = jnp.concatenate([whole, pltpu.roll(whole, LANES - 24, 1)], axis=0).T
+    turned = whole.T
     here = as_tile(image)
-    tv = total_variation(here, turned[0:8], turned[64:72], vox == 0, vox == OWNERS - 1)
+    tv = total_variation(here, turned[32:40], turned[64:72], vox == 0, vox == OWNERS - 1)
     out = here - (STEP_SIZE * TV_WEIGHT) * tv
     for y in range(2):
         for t in range(4):
@@ -287,8 +269,8 @@
     for k in range(K_MAX):
         block = ids[0, 0, k]
         for q in range(4):
-            strip = got[4 * block + q].astype(jnp.float32)
-            wins[k, 2 * q : 2 * q + 2, :] = strip[2 * k : 2 * k + 2, :]
+            strip = got[4 * block + q, :, k * LANES : (k + 1) * LANES]
+            wins[k, 2 * q : 2 * q + 2, :] = strip.astype(jnp.float32)
     windows = []
     for k in range(K_MAX):
         low = lax.rem(starts[0, 0, k], WIN)
@@ -344,7 +326,7 @@
     sent, spread, held = pl.pallas_call(
         forward_kernel,
         out_shape=(
-            jax.ShapeDtypeStruct((OWNERS, ROWS, LANES), jnp.bfloat16),
+            jax.ShapeDtypeStruct((OWNERS, 2, WIDTH), jnp.bfloat16),
             jax.ShapeDtypeStruct((64, LANES), jnp.float32),
             jax.ShapeDtypeStruct((K_MAX, VOXELS, CELLS), jnp.bfloat16),
         ),
@@ -355,8 +337,7 @@
             pltpu.SMEM((1, 1, K_MAX), jnp.int32),
             pltpu.VMEM((1, 2, 512), jnp.float32),
             pltpu.VMEM((1, 4, 2048), jnp.bfloat16),
-            pltpu.VMEM((4, ROWS, LANES), jnp.float32),
-            pltpu.VMEM((OWNERS, LANES), jnp.float32),
+            pltpu.VMEM((2 * OWNERS, LANES), jnp.float32),
             pltpu.SemaphoreType.DMA((4,)),
             pltpu.SemaphoreType.DMA((K_MAX,)),
         ],
@@ -374,12 +355,12 @@
     sent, residual = pl.pallas_call(
         owner_kernel,
         out_shape=(
-            jax.ShapeDtypeStruct((OWNERS, ROWS, LANES), jnp.bfloat16),
+            jax.ShapeDtypeStruct((OWNERS, 2, WIDTH), jnp.bfloat16),
             jax.ShapeDtypeStruct((1, 4, 2048), jnp.float32),
         ),
         in_specs=[vmem(), vmem()],
         out_specs=(vmem(), vmem()),
-        scratch_shapes=[pltpu.VMEM((OWNERS * ROWS, LANES), jnp.float32)],
+        scratch_shapes=[pltpu.VMEM((2 * OWNERS, WIDTH), jnp.float32)],
         compiler_params=pltpu.CompilerParams(vmem_limit_bytes=8 * MIB),
         name="owner",
     )(got, spread)
@@ -400,7 +381,7 @@
         out_shape=jax.ShapeDtypeStruct((1, 2, 512), jnp.float32),
         in_specs=[vmem(), vmem()],
         out_specs=vmem(),
-        scratch_shapes=[pltpu.VMEM((OWNERS * 8, LANES), jnp.float32)],
+        scratch_shapes=[pltpu.VMEM((2 * OWNERS, LANES), jnp.float32)],
         compiler_params=pltpu.CompilerParams(vmem_limit_bytes=8 * MIB),
         cost_estimate=pl.CostEstimate(flops=100000, bytes_accessed=1 << 19, transcendentals=4096),
         name="smooth",

time: 61.5 us -> 58.8 us (0.956)
  blocking collectives: 39.6 us -> 37.8 us
  starting transfers between devices: 7.77 us -> 6.97 us
    all_to_all x2, blocking collectives: 39.6 us -> 37.8 us  [on_device(): got = lax.all_to_all(sent, VOX, 0, 0, tiled=True)]
    ppermute x1, starting transfers between devices: 3.55 us -> 2.76 us  [on_device(): grad = grad + lax.ppermute(grad, 'core', [(0, 1), (1, 0)])]
where the time goes in v4:
time: 58.8 us; the launch traced here: 58.6 us
  blocking collectives  37.8 us (64%)
  Pallas kernels  9.13 us (16%)
  starting transfers between devices  6.97 us (12%)
  waiting for transfers between devices  2.71 us (5%)
  between operations  1.34 us (2%)
  other arithmetic  0.6 us (1%)
    all_to_all x2, blocking collectives, on_device(): got = lax.all_to_all(sent, VOX, 0, 0, tiled=True)  37.8 us
    pallas_call x1, Pallas kernels, on_device(): pl.pallas_call(forward_kernel, out_shape=(jax.ShapeDtypeStruct((OWNERS, 2...  5.11 us
    ppermute x1, starting transfers between devices, on_device(): other = lax.ppermute(grad, 'z_hi', [(0, 1), (1, 0)])  4.21 us
    ppermute x1, starting transfers between devices, on_device(): grad = grad + lax.ppermute(grad, 'core', [(0, 1), (1, 0)])  2.76 us
    pallas_call x1, Pallas kernels, on_device(): pl.pallas_call(backward_kernel, out_shape=jax.ShapeDtypeStruct((1, 2, 512...  2.34 us
    ppermute x1, waiting for transfers between devices, on_device(): other = lax.ppermute(grad, 'z_hi', [(0, 1), (1, 0)])  1.88 us
    pallas_call x1, Pallas kernels, on_device(): pl.pallas_call(owner_kernel, out_shape=(jax.ShapeDtypeStruct((OWNERS, 2,...  1.41 us
  transfers between devices with their start and end apart: 2, of which 2 were waited for; matrix products, arithmetic and copies ran while one was open for 0% of the time, Pallas kernels for 0%

profile of v4, /device:TPU:1, one launch (start us, length us, event | category | flops | bytes accessed | tf_op | source)
XLA Modules:
  0.0 58.6 jit_solution(525811826077009791)
XLA Ops:
  0.6 0.0 copy-start.2
  0.6 0.0 copy-start.1
  1.3 0.0 copy-start
  1.3 5.1 %forward.1 = (bf16[64,2,768]{2,1,0:T(2,128)(2,1)S(1)}, f32[64,128]{1,0:T(8,128)S(1)}, bf16[5,1024,1024]{2,1,0:T(8,128)(2,1)S(1)}) custom-call(s32[1,1,5]{2,1,0:T(1,128)} %ids.1, s32[1,1,5]{2,1,0:T(1,128)} %starts.1, s32[1,1]{1,0:T(1,128)S(6)} %copy.8.counts, f32[1,2,512]{2,1,0:T(2,128)} %image.1, bf16[1,1,5,1024,1024]{4,3,2,1,0:T(8,128)(2,1)} %weights.1, ...), custom_call_target="tpu_custom_call" | custom-call | tf_op jit(solution)/shard_map/forward/pallas_call | solution.py:326
  6.4 22.4 %all_to_all.10.got = bf16[64,2,768]{2,1,0:T(2,128)(2,1)S(1)} all-to-all(bf16[64,2,768]{2,1,0:T(2,128)(2,1)S(1)} %get-tuple-element.7), channel_id=1, replica_groups=mesh['y'=4,'x'=4,'z_lo'=4,'z_hi'=2,'core'=2] {'y','x','z_lo'}, dimensions={0} | all-to-all | bytes 393216 | tf_op jit(solution)/shard_map/all_to_all | solution.py:354
  28.9 1.4 %owner.1 = (bf16[64,2,768]{2,1,0:T(2,128)(2,1)S(1)}, f32[1,4,2048]{2,1,0:T(4,128)}) custom-call(bf16[64,2,768]{2,1,0:T(2,128)(2,1)S(1)} %all_to_all.10.got, f32[64,128]{1,0:T(8,128)S(1)} %get-tuple-element.8.spread), custom_call_target="tpu_custom_call" | custom-call | tf_op jit(solution)/shard_map/owner/pallas_call | solution.py:355
  30.3 15.4 %all_to_all.11.got = bf16[64,2,768]{2,1,0:T(2,128)(2,1)S(1)} all-to-all(bf16[64,2,768]{2,1,0:T(2,128)(2,1)S(1)} %get-tuple-element.9), channel_id=1, replica_groups=mesh['y'=4,'x'=4,'z_lo'=4,'z_hi'=2,'core'=2] {'y','x','z_lo'}, dimensions={0} | all-to-all | bytes 393216 | tf_op jit(solution)/shard_map/all_to_all | solution.py:367
  45.7 0.0 copy-done.2
  45.7 0.0 copy-done.1
  45.7 2.3 %backward.1 = f32[1,2,512]{2,1,0:T(2,128)S(1)} custom-call(s32[1,1,5]{2,1,0:T(1,128)S(1)} %copy-done.1, s32[1,1,5]{2,1,0:T(1,128)S(1)} %copy-done.2, s32[1,1]{1,0:T(1,128)S(6)} %copy.8.counts, bf16[64,2,768]{2,1,0:T(2,128)(2,1)S(1)} %all_to_all.11.got, bf16[5,1024,1024]{2,1,0:T(8,128)(2,1)S(1)} %get-tuple-element.10.held), custom_call_target="tpu_custom_call" | custom-call | tf_op jit(solution)/shard_map/backward/pallas_call | solution.py:368
  48.0 2.8 %collective-permute-start = (f32[1,2,512]{2,1,0:T(2,128)S(1)}, f32[1,2,512]{2,1,0:T(2,128)S(1)}, u32[]{:S(2)}, u32[]{:S(2)}) collective-permute-start(f32[1,2,512]{2,1,0:T(2,128)S(1)} %backward.1), channel_id=1, source_target_pairs={{0,1},{1,0},{2,3},{3,2},{4,5},{5,4},{6,7},{7,6},{8,9},{9,8},{10,11... | collective-permute-start | bytes 12296 | tf_op jit(solution)/shard_map/ppermute | solution.py:377
  50.8 0.8 %collective-permute-done = f32[1,2,512]{2,1,0:T(2,128)S(1)} collective-permute-done((f32[1,2,512]{2,1,0:T(2,128)S(1)}, f32[1,2,512]{2,1,0:T(2,128)S(1)}, u32[]{:S(2)}, u32[]{:S(2)}) %collective-permute-start) | collective-permute-done | bytes 4128 | tf_op jit(solution)/shard_map/ppermute | solution.py:377
  51.6 4.2 %collective-permute-start.1 = (f32[1,2,512]{2,1,0:T(2,128)S(1)}, f32[1,2,512]{2,1,0:T(2,128)S(1)}, u32[]{:S(2)}, u32[]{:S(2)}) collective-permute-start(f32[1,2,512]{2,1,0:T(2,128)S(1)} %add.6), channel_id=1, source_target_pairs={{0,2},{2,0},{1,3},{3,1},{4,6},{6,4},{5,7},{7,5},{8,10},{10,8},{9,1... | collective-permute-start | bytes 12296 | tf_op jit(solution)/shard_map/ppermute | solution.py:378
  55.8 0.0 copy-done
  55.8 0.3 smooth.1
  56.1 1.9 %collective-permute-done.1 = f32[1,2,512]{2,1,0:T(2,128)S(1)} collective-permute-done((f32[1,2,512]{2,1,0:T(2,128)S(1)}, f32[1,2,512]{2,1,0:T(2,128)S(1)}, u32[]{:S(2)}, u32[]{:S(2)}) %collective-permute-start.1) | collective-permute-done | bytes 4128 | tf_op jit(solution)/shard_map/ppermute | solution.py:378
  58.0 0.6 %multiply_subtract_fusion = f32[1,2,512]{2,1,0:T(2,128)} fusion(f32[1,2,512]{2,1,0:T(2,128)S(1)} %smooth.1, f32[1,2,512]{2,1,0:T(2,128)S(1)} %add.6, f32[1,2,512]{2,1,0:T(2,128)S(1)} %collective-permute-done.1), kind=kLoop, calls=%fused_computation | loop fusion | flops 3072 | bytes 16384 | tf_op jit(solution)/shard_map/sub | solution.py:389
  (1 shorter events, 0.0 us)
Async XLA Ops:
  0.6 45.1 %copy-start.2 = (s32[1,1,5]{2,1,0:T(1,128)S(1)}, s32[1,1,5]{2,1,0:T(1,128)}, u32[]{:S(2)}) copy-start(s32[1,1,5]{2,1,0:T(1,128)} %starts.1) | copy-start | bytes 64
  0.6 45.0 %copy-start.1 = (s32[1,1,5]{2,1,0:T(1,128)S(1)}, s32[1,1,5]{2,1,0:T(1,128)}, u32[]{:S(2)}) copy-start(s32[1,1,5]{2,1,0:T(1,128)} %ids.1) | copy-start | bytes 64
  1.3 54.5 %copy-start = (f32[1,2,512]{2,1,0:T(2,128)S(1)}, f32[1,2,512]{2,1,0:T(2,128)}, u32[]{:S(2)}) copy-start(f32[1,2,512]{2,1,0:T(2,128)} %image.1) | copy-start | bytes 12292
  48.0 3.6 %collective-permute-start = (f32[1,2,512]{2,1,0:T(2,128)S(1)}, f32[1,2,512]{2,1,0:T(2,128)S(1)}, u32[]{:S(2)}, u32[]{:S(2)}) collective-permute-start(f32[1,2,512]{2,1,0:T(2,128)S(1)} %backward.1), channel_id=1, source_target_pairs={{0,1},{1,0},{2,3},{3,2},{4,5},{5,4},{6,7},{7,6},{8,9},{9,8},{10,11... | collective-permute-start | bytes 12296 | tf_op jit(solution)/shard_map/ppermute | solution.py:377
  51.6 6.4 %collective-permute-start.1 = (f32[1,2,512]{2,1,0:T(2,128)S(1)}, f32[1,2,512]{2,1,0:T(2,128)S(1)}, u32[]{:S(2)}, u32[]{:S(2)}) collective-permute-start(f32[1,2,512]{2,1,0:T(2,128)S(1)} %add.6), channel_id=1, source_target_pairs={{0,2},{2,0},{1,3},{3,1},{4,6},{6,4},{5,7},{7,5},{8,10},{10,8},{9,1... | collective-permute-start | bytes 12296 | tf_op jit(solution)/shard_map/ppermute | solution.py:378

commit v5 on v4

--- a/solution.py
+++ b/solution.py
@@ -19,6 +19,8 @@
 OWNERS = 64
 ON_MATRIX = 2
 IN_FLIGHT = 3
+PLACE = 2048
+LIVE = 16 * PLACE
 STEP_SIZE = 0.25
 TV_WEIGHT = 0.3
 TV_EPS = 0.01
@@ -57,6 +59,7 @@
     sent,
     spread,
     held,
+    places,
     ids,
     starts,
     image,
@@ -99,8 +102,11 @@
     code_row = base
     block_row = jnp.full((2, LANES), -1, jnp.int32)
     live = counts[0, 0]
+    table = jnp.zeros((8, LANES), jnp.int32)
     for k in range(K_MAX):
         start = starts[0, 0, k]
+        place = start + ids[0, 0, k] * PLACE + jnp.where(k < live, LIVE, 0)
+        table = jnp.where(lane_iota((8, LANES)) == k, place, table)
         coarse = start // WIN
         low = start - coarse * WIN
         code = (coarse & 1) * 16 + (coarse >> 1)
@@ -108,6 +114,7 @@
         base = jnp.where(lane2 == 8 + k, low.astype(jnp.float32), base)
         code_row = jnp.where(lane2 == k, code.astype(jnp.float32), code_row)
         block_row = jnp.where(lane2 == k, block, block_row)
+    places[...] = table
     for b in range(16):
         marked = jnp.where(block_row == b, code_row, base)
         for d in range(4 * b, 4 * b + 4):
@@ -150,7 +157,7 @@
     return ((behind(2) - ahead(2)) + 8.0 * (ahead(1) - behind(1))) * (1.0 / 12.0)
 
 
-def owner_kernel(got, spread, sent, residual, wide):
+def owner_kernel(got, spread, sent, resid, wide):
     for d in range(OWNERS):
         wide[2 * d : 2 * d + 2, :] = got[d].astype(jnp.float32)
     lane = lane_iota((LANES, LANES))
@@ -187,8 +194,9 @@
         rows.append(jnp.where(lane16, even, pltpu.roll(odd, WIN, 1)))
         rows.append(jnp.where(lane16, pltpu.roll(even, WIN, 1), odd))
     signals = jnp.concatenate(rows, axis=0)
-    resid = derivative(signals) - spread[...]
-    adjoint = -derivative(resid)
+    difference = derivative(signals) - spread[...]
+    resid[...] = difference
+    adjoint = -derivative(difference)
     zero = jnp.zeros((32, LANES), jnp.float32)
     table = []
     for u in range(2):
@@ -217,11 +225,6 @@
     )
     for d in range(OWNERS):
         sent[d] = wide[2 * d : 2 * d + 2, :].astype(jnp.bfloat16)
-    for r in range(4):
-        for h in range(16):
-            residual[0, r : r + 1, h * LANES : (h + 1) * LANES] = resid[
-                r * 16 + h : r * 16 + h + 1, :
-            ]
 
 
 def total_variation(image, before, after, is_first, is_last):
@@ -248,7 +251,12 @@
     return result + (jnp.where(first_x, 0.0, moved) - unit_x)
 
 
-def smooth_kernel(got, image, base, wide):
+def smooth_kernel(got, image, resid, base, residual, wide):
+    for r in range(4):
+        for h in range(16):
+            residual[0, r : r + 1, h * LANES : (h + 1) * LANES] = resid[
+                r * 16 + h : r * 16 + h + 1, :
+            ]
     vox = lax.axis_index(VOX)
     for d in range(OWNERS):
         wide[2 * d : 2 * d + 2, :] = got[d, :, K_MAX * LANES :].astype(jnp.float32)
@@ -263,24 +271,24 @@
             base[0, y : y + 1, t * LANES : (t + 1) * LANES] = out[y * 4 + t : y * 4 + t + 1]
 
 
-def backward_kernel(ids, starts, counts, got, held, grad, wins):
-    live = counts[0, 0]
+def backward_kernel(table, got, held, grad, wins):
     lane = lane_iota((8, LANES))
-    for k in range(K_MAX):
-        block = ids[0, 0, k]
+    places = [table[0, k] for k in range(K_MAX)]
+    for k in range(K_MAX):
+        block = (places[k] >> 11) & 15
         for q in range(4):
             strip = got[4 * block + q, :, k * LANES : (k + 1) * LANES]
             wins[k, 2 * q : 2 * q + 2, :] = strip.astype(jnp.float32)
     windows = []
     for k in range(K_MAX):
-        low = lax.rem(starts[0, 0, k], WIN)
+        low = places[k] & (WIN - 1)
         tile = wins[k]
         tile = jnp.where(
             (lane & (WIN - 1)) < WIN - low,
             pltpu.roll(tile, lax.rem(LANES - low, LANES), 1),
             pltpu.roll(tile, WIN - low, 1),
         )
-        windows.append(jnp.where(k < live, tile, 0.0))
+        windows.append(jnp.where(places[k] >= LIVE, tile, 0.0))
     vectors = [
         jnp.concatenate([windows[k][i : i + 1, :] for i in range(8)], axis=1).astype(jnp.bfloat16)
         for k in range(ON_MATRIX)
@@ -323,15 +331,16 @@
 
 
 def on_device(image, weights, block_ids, offsets, counts, measured):
-    sent, spread, held = pl.pallas_call(
+    sent, spread, held, places = pl.pallas_call(
         forward_kernel,
         out_shape=(
             jax.ShapeDtypeStruct((OWNERS, 2, WIDTH), jnp.bfloat16),
             jax.ShapeDtypeStruct((64, LANES), jnp.float32),
             jax.ShapeDtypeStruct((K_MAX, VOXELS, CELLS), jnp.bfloat16),
+            jax.ShapeDtypeStruct((8, LANES), jnp.int32),
         ),
         in_specs=[hbm(), hbm(), smem(), hbm(), hbm(), hbm()],
-        out_specs=(vmem(), vmem(), vmem()),
+        out_specs=(vmem(),) * 4,
         scratch_shapes=[
             pltpu.SMEM((1, 1, K_MAX), jnp.int32),
             pltpu.SMEM((1, 1, K_MAX), jnp.int32),
@@ -352,11 +361,11 @@
         in_hbm(measured),
     )
     got = lax.all_to_all(sent, VOX, 0, 0, tiled=True)
-    sent, residual = pl.pallas_call(
+    sent, resid = pl.pallas_call(
         owner_kernel,
         out_shape=(
             jax.ShapeDtypeStruct((OWNERS, 2, WIDTH), jnp.bfloat16),
-            jax.ShapeDtypeStruct((1, 4, 2048), jnp.float32),
+            jax.ShapeDtypeStruct((64, LANES), jnp.float32),
         ),
         in_specs=[vmem(), vmem()],
         out_specs=(vmem(), vmem()),
@@ -368,24 +377,27 @@
     grad = pl.pallas_call(
         backward_kernel,
         out_shape=jax.ShapeDtypeStruct((1, 2, 512), jnp.float32),
-        in_specs=[smem(), smem(), smem(), vmem(), vmem()],
+        in_specs=[vmem(), vmem(), vmem()],
         out_specs=vmem(),
         scratch_shapes=[pltpu.VMEM((K_MAX, 8, LANES), jnp.float32)],
         compiler_params=pltpu.CompilerParams(vmem_limit_bytes=20 * MIB),
         name="backward",
-    )(block_ids, offsets, counts, got, held)
+    )(places, got, held)
     grad = grad + lax.ppermute(grad, "core", [(0, 1), (1, 0)])
     other = lax.ppermute(grad, "z_hi", [(0, 1), (1, 0)])
-    base = pl.pallas_call(
+    base, residual = pl.pallas_call(
         smooth_kernel,
-        out_shape=jax.ShapeDtypeStruct((1, 2, 512), jnp.float32),
-        in_specs=[vmem(), vmem()],
-        out_specs=vmem(),
+        out_shape=(
+            jax.ShapeDtypeStruct((1, 2, 512), jnp.float32),
+            jax.ShapeDtypeStruct((1, 4, 2048), jnp.float32),
+        ),
+        in_specs=[vmem(), vmem(), vmem()],
+        out_specs=(vmem(), vmem()),
         scratch_shapes=[pltpu.VMEM((2 * OWNERS, LANES), jnp.float32)],
         compiler_params=pltpu.CompilerParams(vmem_limit_bytes=8 * MIB),
         cost_estimate=pl.CostEstimate(flops=100000, bytes_accessed=1 << 19, transcendentals=4096),
         name="smooth",
-    )(got, image)
+    )(got, image, resid)
     return (base - STEP_SIZE * (grad + other), residual)
 
 

time: 58.8 us -> 58.2 us (0.990)
  transfers between devices with their start and end apart: 2 -> 2, of which waited for: 2 -> 2; matrix products, arithmetic and copies ran while one was open for 0% -> 0% of each run, Pallas kernels for 0% -> 1%
where the time goes in v5:
time: 58.2 us; the launch traced here: 58.1 us
  blocking collectives  37.8 us (65%)
  Pallas kernels  9.2 us (16%)
  starting transfers between devices  6.95 us (12%)
  waiting for transfers between devices  2.17 us (4%)
  between operations  1.31 us (2%)
  other arithmetic  0.6 us (1%)
    all_to_all x2, blocking collectives, on_device(): got = lax.all_to_all(sent, VOX, 0, 0, tiled=True)  37.8 us
    pallas_call x1, Pallas kernels, on_device(): pl.pallas_call(forward_kernel, out_shape=(jax.ShapeDtypeStruct((OWNERS, 2...  5.11 us
    ppermute x1, starting transfers between devices, on_device(): other = lax.ppermute(grad, 'z_hi', [(0, 1), (1, 0)])  4.21 us
    ppermute x1, starting transfers between devices, on_device(): grad = grad + lax.ppermute(grad, 'core', [(0, 1), (1, 0)])  2.74 us
    pallas_call x1, Pallas kernels, on_device(): pl.pallas_call(backward_kernel, out_shape=jax.ShapeDtypeStruct((1, 2, 512...  2.01 us
    ppermute x1, waiting for transfers between devices, on_device(): other = lax.ppermute(grad, 'z_hi', [(0, 1), (1, 0)])  1.34 us
    pallas_call x1, Pallas kernels, on_device(): pl.pallas_call(owner_kernel, out_shape=(jax.ShapeDtypeStruct((OWNERS, 2,...  1.26 us
  transfers between devices with their start and end apart: 2, of which 2 were waited for; matrix products, arithmetic and copies ran while one was open for 0% of the time, Pallas kernels for 1%

profile of v5, /device:TPU:1, one launch (start us, length us, event | category | flops | bytes accessed | tf_op | source)
XLA Modules:
  0.0 58.1 jit_solution(3731675889526380966)
XLA Ops:
  1.3 0.0 copy-start
  1.3 5.1 %forward.1 = (bf16[64,2,768]{2,1,0:T(2,128)(2,1)S(1)}, f32[64,128]{1,0:T(8,128)S(1)}, bf16[5,1024,1024]{2,1,0:T(8,128)(2,1)S(1)}, s32[8,128]{1,0:T(8,128)S(1)}) custom-call(s32[1,1,5]{2,1,0:T(1,128)} %ids_hbm.1, s32[1,1,5]{2,1,0:T(1,128)} %starts_hbm.1, s32[1,1]{1,0:T(1,128)S(6)} %copy.8.counts, f32[1,2,512]{2,1,0:T(2,128)} %image.1, ...), custom_call_target="tpu_custom_call" | custom-call | tf_op jit(solution)/shard_map/forward/pallas_call | solution.py:334
  6.4 22.4 %all_to_all.10.got = bf16[64,2,768]{2,1,0:T(2,128)(2,1)S(1)} all-to-all(bf16[64,2,768]{2,1,0:T(2,128)(2,1)S(1)} %get-tuple-element.10), channel_id=1, replica_groups=mesh['y'=4,'x'=4,'z_lo'=4,'z_hi'=2,'core'=2] {'y','x','z_lo'}, dimensions={0} | all-to-all | bytes 393216 | tf_op jit(solution)/shard_map/all_to_all | solution.py:363
  28.8 1.3 %owner.1 = (bf16[64,2,768]{2,1,0:T(2,128)(2,1)S(1)}, f32[64,128]{1,0:T(8,128)S(1)}) custom-call(bf16[64,2,768]{2,1,0:T(2,128)(2,1)S(1)} %all_to_all.10.got, f32[64,128]{1,0:T(8,128)S(1)} %get-tuple-element.11.spread), custom_call_target="tpu_custom_call" | custom-call | tf_op jit(solution)/shard_map/owner/pallas_call | solution.py:364
  30.1 15.4 %all_to_all.11.got = bf16[64,2,768]{2,1,0:T(2,128)(2,1)S(1)} all-to-all(bf16[64,2,768]{2,1,0:T(2,128)(2,1)S(1)} %get-tuple-element.12), channel_id=1, replica_groups=mesh['y'=4,'x'=4,'z_lo'=4,'z_hi'=2,'core'=2] {'y','x','z_lo'}, dimensions={0} | all-to-all | bytes 393216 | tf_op jit(solution)/shard_map/all_to_all | solution.py:376
  45.5 2.0 %backward.1 = f32[1,2,512]{2,1,0:T(2,128)S(1)} custom-call(s32[8,128]{1,0:T(8,128)S(1)} %get-tuple-element.15.table, bf16[64,2,768]{2,1,0:T(2,128)(2,1)S(1)} %all_to_all.11.got, bf16[5,1024,1024]{2,1,0:T(8,128)(2,1)S(1)} %get-tuple-element.16.held), custom_call_target="tpu_custom_call" | custom-call | tf_op jit(solution)/shard_map/backward/pallas_call | solution.py:377
  47.5 2.7 %collective-permute-start = (f32[1,2,512]{2,1,0:T(2,128)S(1)}, f32[1,2,512]{2,1,0:T(2,128)S(1)}, u32[]{:S(2)}, u32[]{:S(2)}) collective-permute-start(f32[1,2,512]{2,1,0:T(2,128)S(1)} %backward.1), channel_id=1, source_target_pairs={{0,1},{1,0},{2,3},{3,2},{4,5},{5,4},{6,7},{7,6},{8,9},{9,8},{10,11... | collective-permute-start | bytes 12296 | tf_op jit(solution)/shard_map/ppermute | solution.py:386
  50.3 0.8 %collective-permute-done = f32[1,2,512]{2,1,0:T(2,128)S(1)} collective-permute-done((f32[1,2,512]{2,1,0:T(2,128)S(1)}, f32[1,2,512]{2,1,0:T(2,128)S(1)}, u32[]{:S(2)}, u32[]{:S(2)}) %collective-permute-start) | collective-permute-done | bytes 4128 | tf_op jit(solution)/shard_map/ppermute | solution.py:386
  51.1 4.2 %collective-permute-start.1 = (f32[1,2,512]{2,1,0:T(2,128)S(1)}, f32[1,2,512]{2,1,0:T(2,128)S(1)}, u32[]{:S(2)}, u32[]{:S(2)}) collective-permute-start(f32[1,2,512]{2,1,0:T(2,128)S(1)} %add.6), channel_id=1, source_target_pairs={{0,2},{2,0},{1,3},{3,1},{4,6},{6,4},{5,7},{7,5},{8,10},{10,8},{9,1... | collective-permute-start | bytes 12296 | tf_op jit(solution)/shard_map/ppermute | solution.py:387
  55.3 0.0 copy-done
  55.3 0.8 %smooth.1 = (f32[1,2,512]{2,1,0:T(2,128)S(1)}, f32[1,4,2048]{2,1,0:T(4,128)}) custom-call(bf16[64,2,768]{2,1,0:T(2,128)(2,1)S(1)} %all_to_all.11.got, f32[1,2,512]{2,1,0:T(2,128)S(1)} %copy-done, f32[64,128]{1,0:T(8,128)S(1)} %get-tuple-element.13.resid), custom_call_target="tpu_custom_call" | custom-call | flops 100000 | bytes 524288 | tf_op jit(solution)/shard_map/smooth/pallas_call | solution.py:388
  56.1 1.3 %collective-permute-done.1 = f32[1,2,512]{2,1,0:T(2,128)S(1)} collective-permute-done((f32[1,2,512]{2,1,0:T(2,128)S(1)}, f32[1,2,512]{2,1,0:T(2,128)S(1)}, u32[]{:S(2)}, u32[]{:S(2)}) %collective-permute-start.1) | collective-permute-done | bytes 4128 | tf_op jit(solution)/shard_map/ppermute | solution.py:387
  57.5 0.6 %multiply_subtract_fusion = f32[1,2,512]{2,1,0:T(2,128)} fusion(f32[1,2,512]{2,1,0:T(2,128)S(1)} %get-tuple-element.14, f32[1,2,512]{2,1,0:T(2,128)S(1)} %add.6, f32[1,2,512]{2,1,0:T(2,128)S(1)} %collective-permute-done.1), kind=kLoop, calls=%fused_computation | loop fusion | flops 3072 | bytes 16384 | tf_op jit(solution)/shard_map/sub | solution.py:401
  (1 shorter events, 0.0 us)
Async XLA Ops:
  1.3 54.0 %copy-start = (f32[1,2,512]{2,1,0:T(2,128)S(1)}, f32[1,2,512]{2,1,0:T(2,128)}, u32[]{:S(2)}) copy-start(f32[1,2,512]{2,1,0:T(2,128)} %image.1) | copy-start | bytes 12292
  47.5 3.6 %collective-permute-start = (f32[1,2,512]{2,1,0:T(2,128)S(1)}, f32[1,2,512]{2,1,0:T(2,128)S(1)}, u32[]{:S(2)}, u32[]{:S(2)}) collective-permute-start(f32[1,2,512]{2,1,0:T(2,128)S(1)} %backward.1), channel_id=1, source_target_pairs={{0,1},{1,0},{2,3},{3,2},{4,5},{5,4},{6,7},{7,6},{8,9},{9,8},{10,11... | collective-permute-start | bytes 12296 | tf_op jit(solution)/shard_map/ppermute | solution.py:386
  51.1 6.4 %collective-permute-start.1 = (f32[1,2,512]{2,1,0:T(2,128)S(1)}, f32[1,2,512]{2,1,0:T(2,128)S(1)}, u32[]{:S(2)}, u32[]{:S(2)}) collective-permute-start(f32[1,2,512]{2,1,0:T(2,128)S(1)} %add.6), channel_id=1, source_target_pairs={{0,2},{2,0},{1,3},{3,1},{4,6},{6,4},{5,7},{7,5},{8,10},{10,8},{9,1... | collective-permute-start | bytes 12296 | tf_op jit(solution)/shard_map/ppermute | solution.py:387

commit v6 on v5

--- a/solution.py
+++ b/solution.py
@@ -18,7 +18,7 @@
 WIDTH = TILES * LANES
 OWNERS = 64
 ON_MATRIX = 2
-IN_FLIGHT = 3
+AHEAD = 2
 PLACE = 2048
 LIVE = 16 * PLACE
 STEP_SIZE = 0.25
@@ -82,8 +82,8 @@
     copies = [
         pltpu.make_async_copy(weights.at[0, 0, k], held.at[k], sems.at[k]) for k in range(K_MAX)
     ]
-    for copy in copies[:IN_FLIGHT]:
-        copy.start()
+    for k in range(K_MAX):
+        copies[k].start(priority=0 if k < AHEAD else 1)
     for copy in small:
         copy.wait()
 
@@ -126,8 +126,6 @@
     lane = lane_iota((8, LANES))
     for k in range(K_MAX):
         copies[k].wait()
-        if k + IN_FLIGHT < K_MAX:
-            copies[k + IN_FLIGHT].start()
         piece = jnp.dot(voxels, held[k], preferred_element_type=jnp.float32)
         tile = jnp.concatenate([piece[:, i * LANES : (i + 1) * LANES] for i in range(8)], axis=0)
         low = lax.rem(starts[0, 0, k], WIN)

time: 58.2 us -> 57.8 us (level)
  no operation moved by 1% of the time
where the time goes in v6:
time: 57.8 us; the launch traced here: 57.7 us
  blocking collectives  37.8 us (65%)
  Pallas kernels  8.8 us (15%)
  starting transfers between devices  6.95 us (12%)
  waiting for transfers between devices  2.17 us (4%)
  between operations  1.31 us (2%)
  other arithmetic  0.6 us (1%)
    all_to_all x2, blocking collectives, on_device(): got = lax.all_to_all(sent, VOX, 0, 0, tiled=True)  37.8 us
    pallas_call x1, Pallas kernels, on_device(): pl.pallas_call(forward_kernel, out_shape=(jax.ShapeDtypeStruct((OWNERS, 2...  4.72 us
    ppermute x1, starting transfers between devices, on_device(): other = lax.ppermute(grad, 'z_hi', [(0, 1), (1, 0)])  4.21 us
    ppermute x1, starting transfers between devices, on_device(): grad = grad + lax.ppermute(grad, 'core', [(0, 1), (1, 0)])  2.74 us
    pallas_call x1, Pallas kernels, on_device(): pl.pallas_call(backward_kernel, out_shape=jax.ShapeDtypeStruct((1, 2, 512...  2.01 us
    ppermute x1, waiting for transfers between devices, on_device(): other = lax.ppermute(grad, 'z_hi', [(0, 1), (1, 0)])  1.34 us
    pallas_call x1, Pallas kernels, on_device(): pl.pallas_call(owner_kernel, out_shape=(jax.ShapeDtypeStruct((OWNERS, 2,...  1.26 us
  transfers between devices with their start and end apart: 2, of which 2 were waited for; matrix products, arithmetic and copies ran while one was open for 0% of the time, Pallas kernels for 1%

profile of v6, /device:TPU:1, one launch (start us, length us, event | category | flops | bytes accessed | tf_op | source)
XLA Modules:
  0.0 57.7 jit_solution(10980337499980979774)
XLA Ops:
  1.3 0.0 copy-start
  1.3 4.7 %forward.1 = (bf16[64,2,768]{2,1,0:T(2,128)(2,1)S(1)}, f32[64,128]{1,0:T(8,128)S(1)}, bf16[5,1024,1024]{2,1,0:T(8,128)(2,1)S(1)}, s32[8,128]{1,0:T(8,128)S(1)}) custom-call(s32[1,1,5]{2,1,0:T(1,128)} %ids_hbm.1, s32[1,1,5]{2,1,0:T(1,128)} %starts_hbm.1, s32[1,1]{1,0:T(1,128)S(6)} %copy.8.counts, f32[1,2,512]{2,1,0:T(2,128)} %image.1, ...), custom_call_target="tpu_custom_call" | custom-call | tf_op jit(solution)/shard_map/forward/pallas_call | solution.py:332
  6.0 22.4 %all_to_all.10.got = bf16[64,2,768]{2,1,0:T(2,128)(2,1)S(1)} all-to-all(bf16[64,2,768]{2,1,0:T(2,128)(2,1)S(1)} %get-tuple-element.10), channel_id=1, replica_groups=mesh['y'=4,'x'=4,'z_lo'=4,'z_hi'=2,'core'=2] {'y','x','z_lo'}, dimensions={0} | all-to-all | bytes 393216 | tf_op jit(solution)/shard_map/all_to_all | solution.py:361
  28.4 1.3 %owner.1 = (bf16[64,2,768]{2,1,0:T(2,128)(2,1)S(1)}, f32[64,128]{1,0:T(8,128)S(1)}) custom-call(bf16[64,2,768]{2,1,0:T(2,128)(2,1)S(1)} %all_to_all.10.got, f32[64,128]{1,0:T(8,128)S(1)} %get-tuple-element.11.spread), custom_call_target="tpu_custom_call" | custom-call | tf_op jit(solution)/shard_map/owner/pallas_call | solution.py:362
  29.7 15.4 %all_to_all.11.got = bf16[64,2,768]{2,1,0:T(2,128)(2,1)S(1)} all-to-all(bf16[64,2,768]{2,1,0:T(2,128)(2,1)S(1)} %get-tuple-element.12), channel_id=1, replica_groups=mesh['y'=4,'x'=4,'z_lo'=4,'z_hi'=2,'core'=2] {'y','x','z_lo'}, dimensions={0} | all-to-all | bytes 393216 | tf_op jit(solution)/shard_map/all_to_all | solution.py:374
  45.1 2.0 %backward.1 = f32[1,2,512]{2,1,0:T(2,128)S(1)} custom-call(s32[8,128]{1,0:T(8,128)S(1)} %get-tuple-element.15.table, bf16[64,2,768]{2,1,0:T(2,128)(2,1)S(1)} %all_to_all.11.got, bf16[5,1024,1024]{2,1,0:T(8,128)(2,1)S(1)} %get-tuple-element.16.held), custom_call_target="tpu_custom_call" | custom-call | tf_op jit(solution)/shard_map/backward/pallas_call | solution.py:375
  47.1 2.7 %collective-permute-start = (f32[1,2,512]{2,1,0:T(2,128)S(1)}, f32[1,2,512]{2,1,0:T(2,128)S(1)}, u32[]{:S(2)}, u32[]{:S(2)}) collective-permute-start(f32[1,2,512]{2,1,0:T(2,128)S(1)} %backward.1), channel_id=1, source_target_pairs={{0,1},{1,0},{2,3},{3,2},{4,5},{5,4},{6,7},{7,6},{8,9},{9,8},{10,11... | collective-permute-start | bytes 12296 | tf_op jit(solution)/shard_map/ppermute | solution.py:384
  49.9 0.8 %collective-permute-done = f32[1,2,512]{2,1,0:T(2,128)S(1)} collective-permute-done((f32[1,2,512]{2,1,0:T(2,128)S(1)}, f32[1,2,512]{2,1,0:T(2,128)S(1)}, u32[]{:S(2)}, u32[]{:S(2)}) %collective-permute-start) | collective-permute-done | bytes 4128 | tf_op jit(solution)/shard_map/ppermute | solution.py:384
  50.7 4.2 %collective-permute-start.1 = (f32[1,2,512]{2,1,0:T(2,128)S(1)}, f32[1,2,512]{2,1,0:T(2,128)S(1)}, u32[]{:S(2)}, u32[]{:S(2)}) collective-permute-start(f32[1,2,512]{2,1,0:T(2,128)S(1)} %add.6), channel_id=1, source_target_pairs={{0,2},{2,0},{1,3},{3,1},{4,6},{6,4},{5,7},{7,5},{8,10},{10,8},{9,1... | collective-permute-start | bytes 12296 | tf_op jit(solution)/shard_map/ppermute | solution.py:385
  54.9 0.0 copy-done
  54.9 0.8 %smooth.1 = (f32[1,2,512]{2,1,0:T(2,128)S(1)}, f32[1,4,2048]{2,1,0:T(4,128)}) custom-call(bf16[64,2,768]{2,1,0:T(2,128)(2,1)S(1)} %all_to_all.11.got, f32[1,2,512]{2,1,0:T(2,128)S(1)} %copy-done, f32[64,128]{1,0:T(8,128)S(1)} %get-tuple-element.13.resid), custom_call_target="tpu_custom_call" | custom-call | flops 100000 | bytes 524288 | tf_op jit(solution)/shard_map/smooth/pallas_call | solution.py:386
  55.7 1.3 %collective-permute-done.1 = f32[1,2,512]{2,1,0:T(2,128)S(1)} collective-permute-done((f32[1,2,512]{2,1,0:T(2,128)S(1)}, f32[1,2,512]{2,1,0:T(2,128)S(1)}, u32[]{:S(2)}, u32[]{:S(2)}) %collective-permute-start.1) | collective-permute-done | bytes 4128 | tf_op jit(solution)/shard_map/ppermute | solution.py:385
  57.1 0.6 %multiply_subtract_fusion = f32[1,2,512]{2,1,0:T(2,128)} fusion(f32[1,2,512]{2,1,0:T(2,128)S(1)} %get-tuple-element.14, f32[1,2,512]{2,1,0:T(2,128)S(1)} %add.6, f32[1,2,512]{2,1,0:T(2,128)S(1)} %collective-permute-done.1), kind=kLoop, calls=%fused_computation | loop fusion | flops 3072 | bytes 16384 | tf_op jit(solution)/shard_map/sub | solution.py:399
  (1 shorter events, 0.0 us)
Async XLA Ops:
  1.3 53.6 %copy-start = (f32[1,2,512]{2,1,0:T(2,128)S(1)}, f32[1,2,512]{2,1,0:T(2,128)}, u32[]{:S(2)}) copy-start(f32[1,2,512]{2,1,0:T(2,128)} %image.1) | copy-start | bytes 12292
  47.1 3.6 %collective-permute-start = (f32[1,2,512]{2,1,0:T(2,128)S(1)}, f32[1,2,512]{2,1,0:T(2,128)S(1)}, u32[]{:S(2)}, u32[]{:S(2)}) collective-permute-start(f32[1,2,512]{2,1,0:T(2,128)S(1)} %backward.1), channel_id=1, source_target_pairs={{0,1},{1,0},{2,3},{3,2},{4,5},{5,4},{6,7},{7,6},{8,9},{9,8},{10,11... | collective-permute-start | bytes 12296 | tf_op jit(solution)/shard_map/ppermute | solution.py:384
  50.7 6.4 %collective-permute-start.1 = (f32[1,2,512]{2,1,0:T(2,128)S(1)}, f32[1,2,512]{2,1,0:T(2,128)S(1)}, u32[]{:S(2)}, u32[]{:S(2)}) collective-permute-start(f32[1,2,512]{2,1,0:T(2,128)S(1)} %add.6), channel_id=1, source_target_pairs={{0,2},{2,0},{1,3},{3,1},{4,6},{6,4},{5,7},{7,5},{8,10},{10,8},{9,1... | collective-permute-start | bytes 12296 | tf_op jit(solution)/shard_map/ppermute | solution.py:385

commit v7 on v6

--- a/solution.py
+++ b/solution.py
@@ -119,9 +119,7 @@
         marked = jnp.where(block_row == b, code_row, base)
         for d in range(4 * b, 4 * b + 4):
             own_halo = halo[pl.ds(d, 2, stride=OWNERS), :]
-            sent[d, :, K_MAX * LANES :] = jnp.where(lane2 < 32, marked, own_halo).astype(
-                jnp.bfloat16
-            )
+            sent[d, :, K_MAX * LANES :] = jnp.where(lane2 < 32, marked, own_halo)
 
     lane = lane_iota((8, LANES))
     for k in range(K_MAX):
@@ -133,7 +131,7 @@
             (lane & (WIN - 1)) >= low, pltpu.roll(tile, low, 1), pltpu.roll(tile, low + WIN, 1)
         )
         for q in range(4):
-            strip = tile[2 * q : 2 * q + 2, :].astype(jnp.bfloat16)
+            strip = tile[2 * q : 2 * q + 2, :]
             for b in range(16):
                 sent[4 * b + q, :, k * LANES : (k + 1) * LANES] = strip
 
@@ -157,7 +155,7 @@
 
 def owner_kernel(got, spread, sent, resid, wide):
     for d in range(OWNERS):
-        wide[2 * d : 2 * d + 2, :] = got[d].astype(jnp.float32)
+        wide[2 * d : 2 * d + 2, :] = got[d]
     lane = lane_iota((LANES, LANES))
     parity = lax.broadcasted_iota(jnp.int32, (LANES, LANES), 0) & 1
     within = (lane & (WIN - 1)).astype(jnp.float32)
@@ -179,10 +177,14 @@
             jnp.concatenate([jnp.where(first, strip, 0.0), jnp.where(first, 0.0, strip)], axis=1)
         )
     place = jnp.concatenate(places, axis=0).astype(jnp.bfloat16)
-    strip = jnp.concatenate(strips, axis=0).astype(jnp.bfloat16)
-    both = lax.dot_general(
-        place, strip, (((0,), (0,)), ((), ())), preferred_element_type=jnp.float32
+    strip = jnp.concatenate(split_three(jnp.concatenate(strips, axis=0)), axis=1)
+    parts = lax.dot_general(
+        place,
+        strip.astype(jnp.bfloat16),
+        (((0,), (0,)), ((), ())),
+        preferred_element_type=jnp.float32,
     )
+    both = parts[:, :256] + (parts[:, 256:512] + parts[:, 512:])
     lane16 = lane_iota((16, LANES)) < WIN
     rows = []
     for u in range(2):
@@ -332,7 +334,7 @@
     sent, spread, held, places = pl.pallas_call(
         forward_kernel,
         out_shape=(
-            jax.ShapeDtypeStruct((OWNERS, 2, WIDTH), jnp.bfloat16),
+            jax.ShapeDtypeStruct((OWNERS, 2, WIDTH), jnp.float32),
             jax.ShapeDtypeStruct((64, LANES), jnp.float32),
             jax.ShapeDtypeStruct((K_MAX, VOXELS, CELLS), jnp.bfloat16),
             jax.ShapeDtypeStruct((8, LANES), jnp.int32),

time: 57.8 us -> 62 us (1.073)
  blocking collectives: 37.8 us -> 41.8 us
    all_to_all x2, blocking collectives: 37.8 us -> 41.8 us  [on_device(): got = lax.all_to_all(sent, VOX, 0, 0, tiled=True)]
where the time goes in v7:
time: 62 us; the launch traced here: 61.8 us
  blocking collectives  41.8 us (67%)
  Pallas kernels  9.01 us (15%)
  starting transfers between devices  6.95 us (11%)
  waiting for transfers between devices  2.16 us (3%)
  between operations  1.31 us (2%)
    all_to_all x2, blocking collectives, on_device(): got = lax.all_to_all(sent, VOX, 0, 0, tiled=True)  41.8 us
    pallas_call x1, Pallas kernels, on_device(): pl.pallas_call(forward_kernel, out_shape=(jax.ShapeDtypeStruct((OWNERS, 2...  4.71 us
    ppermute x1, starting transfers between devices, on_device(): other = lax.ppermute(grad, 'z_hi', [(0, 1), (1, 0)])  4.21 us
    ppermute x1, starting transfers between devices, on_device(): grad = grad + lax.ppermute(grad, 'core', [(0, 1), (1, 0)])  2.73 us
    pallas_call x1, Pallas kernels, on_device(): pl.pallas_call(backward_kernel, out_shape=jax.ShapeDtypeStruct((1, 2, 512...  2.01 us
    pallas_call x1, Pallas kernels, on_device(): pl.pallas_call(owner_kernel, out_shape=(jax.ShapeDtypeStruct((OWNERS, 2,...  1.48 us
    ppermute x1, waiting for transfers between devices, on_device(): other = lax.ppermute(grad, 'z_hi', [(0, 1), (1, 0)])  1.34 us
  transfers between devices with their start and end apart: 2, of which 2 were waited for; matrix products, arithmetic and copies ran while one was open for 0% of the time, Pallas kernels for 1%

profile of v7, /device:TPU:1, one launch (start us, length us, event | category | flops | bytes accessed | tf_op | source)
XLA Modules:
  0.0 61.8 jit_solution(15659302193466116063)
XLA Ops:
  1.3 0.0 copy-start
  1.3 4.7 %forward.1 = (f32[64,2,768]{2,1,0:T(2,128)S(1)}, f32[64,128]{1,0:T(8,128)S(1)}, bf16[5,1024,1024]{2,1,0:T(8,128)(2,1)S(1)}, s32[8,128]{1,0:T(8,128)S(1)}) custom-call(s32[1,1,5]{2,1,0:T(1,128)} %ids_hbm.1, s32[1,1,5]{2,1,0:T(1,128)} %starts_hbm.1, s32[1,1]{1,0:T(1,128)S(6)} %copy.8.counts, f32[1,2,512]{2,1,0:T(2,128)} %image.1, ...), custom_call_target="tpu_custom_call" | custom-call | tf_op jit(solution)/shard_map/forward/pallas_call | solution.py:334
  6.0 27.0 %all_to_all.10.got = f32[64,2,768]{2,1,0:T(2,128)S(1)} all-to-all(f32[64,2,768]{2,1,0:T(2,128)S(1)} %get-tuple-element.10), channel_id=1, replica_groups=mesh['y'=4,'x'=4,'z_lo'=4,'z_hi'=2,'core'=2] {'y','x','z_lo'}, dimensions={0} | all-to-all | bytes 786432 | tf_op jit(solution)/shard_map/all_to_all | solution.py:363
  33.0 1.5 %owner.1 = (bf16[64,2,768]{2,1,0:T(2,128)(2,1)S(1)}, f32[64,128]{1,0:T(8,128)S(1)}) custom-call(f32[64,2,768]{2,1,0:T(2,128)S(1)} %all_to_all.10.got, f32[64,128]{1,0:T(8,128)S(1)} %get-tuple-element.11.spread), custom_call_target="tpu_custom_call" | custom-call | tf_op jit(solution)/shard_map/owner/pallas_call | solution.py:364
  34.5 14.8 %all_to_all.11.got = bf16[64,2,768]{2,1,0:T(2,128)(2,1)S(1)} all-to-all(bf16[64,2,768]{2,1,0:T(2,128)(2,1)S(1)} %get-tuple-element.12), channel_id=1, replica_groups=mesh['y'=4,'x'=4,'z_lo'=4,'z_hi'=2,'core'=2] {'y','x','z_lo'}, dimensions={0} | all-to-all | bytes 393216 | tf_op jit(solution)/shard_map/all_to_all | solution.py:376
  49.3 2.0 %backward.1 = f32[1,2,512]{2,1,0:T(2,128)S(1)} custom-call(s32[8,128]{1,0:T(8,128)S(1)} %get-tuple-element.15.table, bf16[64,2,768]{2,1,0:T(2,128)(2,1)S(1)} %all_to_all.11.got, bf16[5,1024,1024]{2,1,0:T(8,128)(2,1)S(1)} %get-tuple-element.16.held), custom_call_target="tpu_custom_call" | custom-call | tf_op jit(solution)/shard_map/backward/pallas_call | solution.py:377
  51.3 2.7 %collective-permute-start = (f32[1,2,512]{2,1,0:T(2,128)S(1)}, f32[1,2,512]{2,1,0:T(2,128)S(1)}, u32[]{:S(2)}, u32[]{:S(2)}) collective-permute-start(f32[1,2,512]{2,1,0:T(2,128)S(1)} %backward.1), channel_id=1, source_target_pairs={{0,1},{1,0},{2,3},{3,2},{4,5},{5,4},{6,7},{7,6},{8,9},{9,8},{10,11... | collective-permute-start | bytes 12296 | tf_op jit(solution)/shard_map/ppermute | solution.py:386
  54.0 0.8 %collective-permute-done = f32[1,2,512]{2,1,0:T(2,128)S(1)} collective-permute-done((f32[1,2,512]{2,1,0:T(2,128)S(1)}, f32[1,2,512]{2,1,0:T(2,128)S(1)}, u32[]{:S(2)}, u32[]{:S(2)}) %collective-permute-start) | collective-permute-done | bytes 4128 | tf_op jit(solution)/shard_map/ppermute | solution.py:386
  54.9 4.2 %collective-permute-start.1 = (f32[1,2,512]{2,1,0:T(2,128)S(1)}, f32[1,2,512]{2,1,0:T(2,128)S(1)}, u32[]{:S(2)}, u32[]{:S(2)}) collective-permute-start(f32[1,2,512]{2,1,0:T(2,128)S(1)} %add.6), channel_id=1, source_target_pairs={{0,2},{2,0},{1,3},{3,1},{4,6},{6,4},{5,7},{7,5},{8,10},{10,8},{9,1... | collective-permute-start | bytes 12296 | tf_op jit(solution)/shard_map/ppermute | solution.py:387
  59.1 0.0 copy-done
  59.1 0.8 %smooth.1 = (f32[1,2,512]{2,1,0:T(2,128)S(1)}, f32[1,4,2048]{2,1,0:T(4,128)}) custom-call(bf16[64,2,768]{2,1,0:T(2,128)(2,1)S(1)} %all_to_all.11.got, f32[1,2,512]{2,1,0:T(2,128)S(1)} %copy-done, f32[64,128]{1,0:T(8,128)S(1)} %get-tuple-element.13.resid), custom_call_target="tpu_custom_call" | custom-call | flops 100000 | bytes 524288 | tf_op jit(solution)/shard_map/smooth/pallas_call | solution.py:388
  59.9 1.3 %collective-permute-done.1 = f32[1,2,512]{2,1,0:T(2,128)S(1)} collective-permute-done((f32[1,2,512]{2,1,0:T(2,128)S(1)}, f32[1,2,512]{2,1,0:T(2,128)S(1)}, u32[]{:S(2)}, u32[]{:S(2)}) %collective-permute-start.1) | collective-permute-done | bytes 4128 | tf_op jit(solution)/shard_map/ppermute | solution.py:387
  61.2 0.6 multiply_subtract_fusion
  (1 shorter events, 0.0 us)
Async XLA Ops:
  1.3 57.8 %copy-start = (f32[1,2,512]{2,1,0:T(2,128)S(1)}, f32[1,2,512]{2,1,0:T(2,128)}, u32[]{:S(2)}) copy-start(f32[1,2,512]{2,1,0:T(2,128)} %image.1) | copy-start | bytes 12292
  51.3 3.6 %collective-permute-start = (f32[1,2,512]{2,1,0:T(2,128)S(1)}, f32[1,2,512]{2,1,0:T(2,128)S(1)}, u32[]{:S(2)}, u32[]{:S(2)}) collective-permute-start(f32[1,2,512]{2,1,0:T(2,128)S(1)} %backward.1), channel_id=1, source_target_pairs={{0,1},{1,0},{2,3},{3,2},{4,5},{5,4},{6,7},{7,6},{8,9},{9,8},{10,11... | collective-permute-start | bytes 12296 | tf_op jit(solution)/shard_map/ppermute | solution.py:386
  54.9 6.4 %collective-permute-start.1 = (f32[1,2,512]{2,1,0:T(2,128)S(1)}, f32[1,2,512]{2,1,0:T(2,128)S(1)}, u32[]{:S(2)}, u32[]{:S(2)}) collective-permute-start(f32[1,2,512]{2,1,0:T(2,128)S(1)} %add.6), channel_id=1, source_target_pairs={{0,2},{2,0},{1,3},{3,1},{4,6},{6,4},{5,7},{7,5},{8,10},{10,8},{9,1... | collective-permute-start | bytes 12296 | tf_op jit(solution)/shard_map/ppermute | solution.py:387

commit v8 on v6

--- a/solution.py
+++ b/solution.py
@@ -156,8 +156,7 @@
 
 
 def owner_kernel(got, spread, sent, resid, wide):
-    for d in range(OWNERS):
-        wide[2 * d : 2 * d + 2, :] = got[d].astype(jnp.float32)
+    wide[...] = got[...].reshape(2 * OWNERS, WIDTH).astype(jnp.float32)
     lane = lane_iota((LANES, LANES))
     parity = lax.broadcasted_iota(jnp.int32, (LANES, LANES), 0) & 1
     within = (lane & (WIN - 1)).astype(jnp.float32)
@@ -165,10 +164,19 @@
     first_half = (lane & 32) == 0
     slot = jnp.where(own_half, lane & 31, -1).astype(jnp.float32)
     info = wide[:, K_MAX * LANES :]
+    shape = (LANES, 2 * K_MAX * LANES)
+    source = lax.broadcasted_iota(jnp.int32, shape, 1) >> 7
+    source = jnp.where(source < K_MAX, source, source + 8 - K_MAX)
+    pick = jnp.where(lax.broadcasted_iota(jnp.int32, shape, 0) == source, 1.0, 0.0)
+    spread_out = jnp.dot(
+        jnp.where(lane < 16, info, 0.0).astype(jnp.bfloat16),
+        pick.astype(jnp.bfloat16),
+        preferred_element_type=jnp.float32,
+    )
     places, strips, later = [], [], []
     for k in range(K_MAX):
-        code = jnp.broadcast_to(info[:, k : k + 1], (LANES, LANES))
-        low = jnp.broadcast_to(info[:, 8 + k : 9 + k], (LANES, LANES))
+        code = spread_out[:, k * LANES : (k + 1) * LANES]
+        low = spread_out[:, (K_MAX + k) * LANES : (K_MAX + k + 1) * LANES]
         following = jnp.where(code >= 16.0, code - 15.0, code + 16.0)
         wanted = jnp.where(first_half, code, following)
         places.append(jnp.where(wanted == slot, 1.0, 0.0))
@@ -221,8 +229,7 @@
         pltpu.roll(info, 2, 0),
         pltpu.roll(pltpu.roll(info, LANES - 2, 0), 32, 1),
     )
-    for d in range(OWNERS):
-        sent[d] = wide[2 * d : 2 * d + 2, :].astype(jnp.bfloat16)
+    sent[...] = wide[...].astype(jnp.bfloat16).reshape(OWNERS, 2, WIDTH)
 
 
 def total_variation(image, before, after, is_first, is_last):
@@ -381,8 +388,8 @@
         compiler_params=pltpu.CompilerParams(vmem_limit_bytes=20 * MIB),
         name="backward",
     )(places, got, held)
-    grad = grad + lax.ppermute(grad, "core", [(0, 1), (1, 0)])
-    other = lax.ppermute(grad, "z_hi", [(0, 1), (1, 0)])
+    grad = grad + lax.ppermute(grad, "z_hi", [(0, 1), (1, 0)])
+    other = lax.ppermute(grad, "core", [(0, 1), (1, 0)])
     base, residual = pl.pallas_call(
         smooth_kernel,
         out_shape=(

time: 57.8 us -> 58.8 us (1.017)
  starting transfers between devices: 6.95 us -> 8.09 us
    ppermute x2, starting transfers between devices: 6.95 us -> 8.09 us  [the longest x1 4.25 us: on_device(): grad = grad + lax.ppermute(grad, 'z_hi', [(0, 1), (1, 0)])]
  transfers between devices with their start and end apart: 2 -> 2, of which waited for: 2 -> 1; matrix products, arithmetic and copies ran while one was open for 0% -> 0% of each run, Pallas kernels for 1% -> 1%
where the time goes in v8:
time: 58.8 us; the launch traced here: 58.7 us
  blocking collectives  37.8 us (64%)
  Pallas kernels  8.64 us (15%)
  starting transfers between devices  8.09 us (14%)
  waiting for transfers between devices  2.16 us (4%)
  between operations  1.31 us (2%)
  other arithmetic  0.6 us (1%)
    all_to_all x2, blocking collectives, on_device(): got = lax.all_to_all(sent, VOX, 0, 0, tiled=True)  37.8 us
    pallas_call x1, Pallas kernels, on_device(): pl.pallas_call(forward_kernel, out_shape=(jax.ShapeDtypeStruct((OWNERS, 2...  4.72 us
    ppermute x1, starting transfers between devices, on_device(): grad = grad + lax.ppermute(grad, 'z_hi', [(0, 1), (1, 0)])  4.25 us
    ppermute x1, starting transfers between devices, on_device(): other = lax.ppermute(grad, 'core', [(0, 1), (1, 0)])  3.85 us
    ppermute x1, waiting for transfers between devices, on_device(): grad = grad + lax.ppermute(grad, 'z_hi', [(0, 1), (1, 0)])  2.15 us
    pallas_call x1, Pallas kernels, on_device(): pl.pallas_call(backward_kernel, out_shape=jax.ShapeDtypeStruct((1, 2, 512...  2.01 us
  transfers between devices with their start and end apart: 2, of which 1 were waited for; matrix products, arithmetic and copies ran while one was open for 0% of the time, Pallas kernels for 1%

profile of v8, /device:TPU:1, one launch (start us, length us, event | category | flops | bytes accessed | tf_op | source)
XLA Modules:
  0.0 58.7 jit_solution(14215736384896848030)
XLA Ops:
  1.3 0.0 copy-start
  1.3 4.7 %forward.1 = (bf16[64,2,768]{2,1,0:T(2,128)(2,1)S(1)}, f32[64,128]{1,0:T(8,128)S(1)}, bf16[5,1024,1024]{2,1,0:T(8,128)(2,1)S(1)}, s32[8,128]{1,0:T(8,128)S(1)}) custom-call(s32[1,1,5]{2,1,0:T(1,128)} %ids_hbm.1, s32[1,1,5]{2,1,0:T(1,128)} %starts_hbm.1, s32[1,1]{1,0:T(1,128)S(6)} %copy.8.counts, f32[1,2,512]{2,1,0:T(2,128)} %image.1, ...), custom_call_target="tpu_custom_call" | custom-call | tf_op jit(solution)/shard_map/forward/pallas_call | solution.py:339
  6.0 22.4 %all_to_all.10.got = bf16[64,2,768]{2,1,0:T(2,128)(2,1)S(1)} all-to-all(bf16[64,2,768]{2,1,0:T(2,128)(2,1)S(1)} %get-tuple-element.10), channel_id=1, replica_groups=mesh['y'=4,'x'=4,'z_lo'=4,'z_hi'=2,'core'=2] {'y','x','z_lo'}, dimensions={0} | all-to-all | bytes 393216 | tf_op jit(solution)/shard_map/all_to_all | solution.py:368
  28.4 1.1 %owner.1 = (bf16[64,2,768]{2,1,0:T(2,128)(2,1)S(1)}, f32[64,128]{1,0:T(8,128)S(1)}) custom-call(bf16[64,2,768]{2,1,0:T(2,128)(2,1)S(1)} %all_to_all.10.got, f32[64,128]{1,0:T(8,128)S(1)} %get-tuple-element.11.spread), custom_call_target="tpu_custom_call" | custom-call | tf_op jit(solution)/shard_map/owner/pallas_call | solution.py:369
  29.5 15.4 %all_to_all.11.got = bf16[64,2,768]{2,1,0:T(2,128)(2,1)S(1)} all-to-all(bf16[64,2,768]{2,1,0:T(2,128)(2,1)S(1)} %get-tuple-element.12), channel_id=1, replica_groups=mesh['y'=4,'x'=4,'z_lo'=4,'z_hi'=2,'core'=2] {'y','x','z_lo'}, dimensions={0} | all-to-all | bytes 393216 | tf_op jit(solution)/shard_map/all_to_all | solution.py:381
  45.0 2.0 %backward.1 = f32[1,2,512]{2,1,0:T(2,128)S(1)} custom-call(s32[8,128]{1,0:T(8,128)S(1)} %get-tuple-element.15.table, bf16[64,2,768]{2,1,0:T(2,128)(2,1)S(1)} %all_to_all.11.got, bf16[5,1024,1024]{2,1,0:T(8,128)(2,1)S(1)} %get-tuple-element.16.held), custom_call_target="tpu_custom_call" | custom-call | tf_op jit(solution)/shard_map/backward/pallas_call | solution.py:382
  47.0 4.2 %collective-permute-start = (f32[1,2,512]{2,1,0:T(2,128)S(1)}, f32[1,2,512]{2,1,0:T(2,128)S(1)}, u32[]{:S(2)}, u32[]{:S(2)}) collective-permute-start(f32[1,2,512]{2,1,0:T(2,128)S(1)} %backward.1), channel_id=1, source_target_pairs={{0,2},{2,0},{1,3},{3,1},{4,6},{6,4},{5,7},{7,5},{8,10},{10,8},{9,1... | collective-permute-start | bytes 12296 | tf_op jit(solution)/shard_map/ppermute | solution.py:391
  51.2 2.2 %collective-permute-done = f32[1,2,512]{2,1,0:T(2,128)S(1)} collective-permute-done((f32[1,2,512]{2,1,0:T(2,128)S(1)}, f32[1,2,512]{2,1,0:T(2,128)S(1)}, u32[]{:S(2)}, u32[]{:S(2)}) %collective-permute-start) | collective-permute-done | bytes 4128 | tf_op jit(solution)/shard_map/ppermute | solution.py:391
  53.4 3.8 %collective-permute-start.1 = (f32[1,2,512]{2,1,0:T(2,128)S(1)}, f32[1,2,512]{2,1,0:T(2,128)S(1)}, u32[]{:S(2)}, u32[]{:S(2)}) collective-permute-start(f32[1,2,512]{2,1,0:T(2,128)S(1)} %add.6), channel_id=1, source_target_pairs={{0,1},{1,0},{2,3},{3,2},{4,5},{5,4},{6,7},{7,6},{8,9},{9,8},{10,11... | collective-permute-start | bytes 12296 | tf_op jit(solution)/shard_map/ppermute | solution.py:392
  57.2 0.0 copy-done
  57.2 0.8 %smooth.1 = (f32[1,2,512]{2,1,0:T(2,128)S(1)}, f32[1,4,2048]{2,1,0:T(4,128)}) custom-call(bf16[64,2,768]{2,1,0:T(2,128)(2,1)S(1)} %all_to_all.11.got, f32[1,2,512]{2,1,0:T(2,128)S(1)} %copy-done, f32[64,128]{1,0:T(8,128)S(1)} %get-tuple-element.13.resid), custom_call_target="tpu_custom_call" | custom-call | flops 100000 | bytes 524288 | tf_op jit(solution)/shard_map/smooth/pallas_call | solution.py:393
  58.0 0.0 collective-permute-done.1
  58.1 0.6 %multiply_subtract_fusion = f32[1,2,512]{2,1,0:T(2,128)} fusion(f32[1,2,512]{2,1,0:T(2,128)S(1)} %get-tuple-element.14, f32[1,2,512]{2,1,0:T(2,128)S(1)} %add.6, f32[1,2,512]{2,1,0:T(2,128)S(1)} %collective-permute-done.1), kind=kLoop, calls=%fused_computation | loop fusion | flops 3072 | bytes 16384 | tf_op jit(solution)/shard_map/sub | solution.py:406
  (1 shorter events, 0.0 us)
Async XLA Ops:
  1.3 56.0 %copy-start = (f32[1,2,512]{2,1,0:T(2,128)S(1)}, f32[1,2,512]{2,1,0:T(2,128)}, u32[]{:S(2)}) copy-start(f32[1,2,512]{2,1,0:T(2,128)} %image.1) | copy-start | bytes 12292
  47.0 6.4 %collective-permute-start = (f32[1,2,512]{2,1,0:T(2,128)S(1)}, f32[1,2,512]{2,1,0:T(2,128)S(1)}, u32[]{:S(2)}, u32[]{:S(2)}) collective-permute-start(f32[1,2,512]{2,1,0:T(2,128)S(1)} %backward.1), channel_id=1, source_target_pairs={{0,2},{2,0},{1,3},{3,1},{4,6},{6,4},{5,7},{7,5},{8,10},{10,8},{9,1... | collective-permute-start | bytes 12296 | tf_op jit(solution)/shard_map/ppermute | solution.py:391
  53.4 4.7 %collective-permute-start.1 = (f32[1,2,512]{2,1,0:T(2,128)S(1)}, f32[1,2,512]{2,1,0:T(2,128)S(1)}, u32[]{:S(2)}, u32[]{:S(2)}) collective-permute-start(f32[1,2,512]{2,1,0:T(2,128)S(1)} %add.6), channel_id=1, source_target_pairs={{0,1},{1,0},{2,3},{3,2},{4,5},{5,4},{6,7},{7,6},{8,9},{9,8},{10,11... | collective-permute-start | bytes 12296 | tf_op jit(solution)/shard_map/ppermute | solution.py:392

commit v9 on v8

--- a/solution.py
+++ b/solution.py
@@ -388,8 +388,8 @@
         compiler_params=pltpu.CompilerParams(vmem_limit_bytes=20 * MIB),
         name="backward",
     )(places, got, held)
-    grad = grad + lax.ppermute(grad, "z_hi", [(0, 1), (1, 0)])
-    other = lax.ppermute(grad, "core", [(0, 1), (1, 0)])
+    grad = grad + lax.ppermute(grad, "core", [(0, 1), (1, 0)])
+    other = lax.ppermute(grad, "z_hi", [(0, 1), (1, 0)])
     base, residual = pl.pallas_call(
         smooth_kernel,
         out_shape=(

time: 58.8 us -> 57.7 us (0.981)
  starting transfers between devices: 8.09 us -> 6.94 us
    ppermute x2, starting transfers between devices: 8.09 us -> 6.94 us  [the longest x1 4.21 us: on_device(): other = lax.ppermute(grad, 'z_hi', [(0, 1), (1, 0)])]
  transfers between devices with their start and end apart: 2 -> 2, of which waited for: 1 -> 2; matrix products, arithmetic and copies ran while one was open for 0% -> 0% of each run, Pallas kernels for 1% -> 1%
where the time goes in v9:
time: 57.7 us; the launch traced here: 57.5 us
  blocking collectives  37.8 us (66%)
  Pallas kernels  8.64 us (15%)
  starting transfers between devices  6.94 us (12%)
  waiting for transfers between devices  2.16 us (4%)
  between operations  1.31 us (2%)
  other arithmetic  0.6 us (1%)
    all_to_all x2, blocking collectives, on_device(): got = lax.all_to_all(sent, VOX, 0, 0, tiled=True)  37.8 us
    pallas_call x1, Pallas kernels, on_device(): pl.pallas_call(forward_kernel, out_shape=(jax.ShapeDtypeStruct((OWNERS, 2...  4.72 us
    ppermute x1, starting transfers between devices, on_device(): other = lax.ppermute(grad, 'z_hi', [(0, 1), (1, 0)])  4.21 us
    ppermute x1, starting transfers between devices, on_device(): grad = grad + lax.ppermute(grad, 'core', [(0, 1), (1, 0)])  2.73 us
    pallas_call x1, Pallas kernels, on_device(): pl.pallas_call(backward_kernel, out_shape=jax.ShapeDtypeStruct((1, 2, 512...  2.01 us
    ppermute x1, waiting for transfers between devices, on_device(): other = lax.ppermute(grad, 'z_hi', [(0, 1), (1, 0)])  1.34 us
  transfers between devices with their start and end apart: 2, of which 2 were waited for; matrix products, arithmetic and copies ran while one was open for 0% of the time, Pallas kernels for 1%

profile of v9, /device:TPU:1, one launch (start us, length us, event | category | flops | bytes accessed | tf_op | source)
XLA Modules:
  0.0 57.5 jit_solution(13370856745755002248)
XLA Ops:
  1.3 0.0 copy-start
  1.3 4.7 %forward.1 = (bf16[64,2,768]{2,1,0:T(2,128)(2,1)S(1)}, f32[64,128]{1,0:T(8,128)S(1)}, bf16[5,1024,1024]{2,1,0:T(8,128)(2,1)S(1)}, s32[8,128]{1,0:T(8,128)S(1)}) custom-call(s32[1,1,5]{2,1,0:T(1,128)} %ids_hbm.1, s32[1,1,5]{2,1,0:T(1,128)} %starts_hbm.1, s32[1,1]{1,0:T(1,128)S(6)} %copy.8.counts, f32[1,2,512]{2,1,0:T(2,128)} %image.1, ...), custom_call_target="tpu_custom_call" | custom-call | tf_op jit(solution)/shard_map/forward/pallas_call | solution.py:339
  6.0 22.4 %all_to_all.10.got = bf16[64,2,768]{2,1,0:T(2,128)(2,1)S(1)} all-to-all(bf16[64,2,768]{2,1,0:T(2,128)(2,1)S(1)} %get-tuple-element.10), channel_id=1, replica_groups=mesh['y'=4,'x'=4,'z_lo'=4,'z_hi'=2,'core'=2] {'y','x','z_lo'}, dimensions={0} | all-to-all | bytes 393216 | tf_op jit(solution)/shard_map/all_to_all | solution.py:368
  28.4 1.1 %owner.1 = (bf16[64,2,768]{2,1,0:T(2,128)(2,1)S(1)}, f32[64,128]{1,0:T(8,128)S(1)}) custom-call(bf16[64,2,768]{2,1,0:T(2,128)(2,1)S(1)} %all_to_all.10.got, f32[64,128]{1,0:T(8,128)S(1)} %get-tuple-element.11.spread), custom_call_target="tpu_custom_call" | custom-call | tf_op jit(solution)/shard_map/owner/pallas_call | solution.py:369
  29.5 15.4 %all_to_all.11.got = bf16[64,2,768]{2,1,0:T(2,128)(2,1)S(1)} all-to-all(bf16[64,2,768]{2,1,0:T(2,128)(2,1)S(1)} %get-tuple-element.12), channel_id=1, replica_groups=mesh['y'=4,'x'=4,'z_lo'=4,'z_hi'=2,'core'=2] {'y','x','z_lo'}, dimensions={0} | all-to-all | bytes 393216 | tf_op jit(solution)/shard_map/all_to_all | solution.py:381
  45.0 2.0 %backward.1 = f32[1,2,512]{2,1,0:T(2,128)S(1)} custom-call(s32[8,128]{1,0:T(8,128)S(1)} %get-tuple-element.15.table, bf16[64,2,768]{2,1,0:T(2,128)(2,1)S(1)} %all_to_all.11.got, bf16[5,1024,1024]{2,1,0:T(8,128)(2,1)S(1)} %get-tuple-element.16.held), custom_call_target="tpu_custom_call" | custom-call | tf_op jit(solution)/shard_map/backward/pallas_call | solution.py:382
  47.0 2.7 %collective-permute-start = (f32[1,2,512]{2,1,0:T(2,128)S(1)}, f32[1,2,512]{2,1,0:T(2,128)S(1)}, u32[]{:S(2)}, u32[]{:S(2)}) collective-permute-start(f32[1,2,512]{2,1,0:T(2,128)S(1)} %backward.1), channel_id=1, source_target_pairs={{0,1},{1,0},{2,3},{3,2},{4,5},{5,4},{6,7},{7,6},{8,9},{9,8},{10,11... | collective-permute-start | bytes 12296 | tf_op jit(solution)/shard_map/ppermute | solution.py:391
  49.7 0.8 %collective-permute-done = f32[1,2,512]{2,1,0:T(2,128)S(1)} collective-permute-done((f32[1,2,512]{2,1,0:T(2,128)S(1)}, f32[1,2,512]{2,1,0:T(2,128)S(1)}, u32[]{:S(2)}, u32[]{:S(2)}) %collective-permute-start) | collective-permute-done | bytes 4128 | tf_op jit(solution)/shard_map/ppermute | solution.py:391
  50.5 4.2 %collective-permute-start.1 = (f32[1,2,512]{2,1,0:T(2,128)S(1)}, f32[1,2,512]{2,1,0:T(2,128)S(1)}, u32[]{:S(2)}, u32[]{:S(2)}) collective-permute-start(f32[1,2,512]{2,1,0:T(2,128)S(1)} %add.6), channel_id=1, source_target_pairs={{0,2},{2,0},{1,3},{3,1},{4,6},{6,4},{5,7},{7,5},{8,10},{10,8},{9,1... | collective-permute-start | bytes 12296 | tf_op jit(solution)/shard_map/ppermute | solution.py:392
  54.7 0.0 copy-done
  54.8 0.8 %smooth.1 = (f32[1,2,512]{2,1,0:T(2,128)S(1)}, f32[1,4,2048]{2,1,0:T(4,128)}) custom-call(bf16[64,2,768]{2,1,0:T(2,128)(2,1)S(1)} %all_to_all.11.got, f32[1,2,512]{2,1,0:T(2,128)S(1)} %copy-done, f32[64,128]{1,0:T(8,128)S(1)} %get-tuple-element.13.resid), custom_call_target="tpu_custom_call" | custom-call | flops 100000 | bytes 524288 | tf_op jit(solution)/shard_map/smooth/pallas_call | solution.py:393
  55.6 1.3 %collective-permute-done.1 = f32[1,2,512]{2,1,0:T(2,128)S(1)} collective-permute-done((f32[1,2,512]{2,1,0:T(2,128)S(1)}, f32[1,2,512]{2,1,0:T(2,128)S(1)}, u32[]{:S(2)}, u32[]{:S(2)}) %collective-permute-start.1) | collective-permute-done | bytes 4128 | tf_op jit(solution)/shard_map/ppermute | solution.py:392
  56.9 0.6 %multiply_subtract_fusion = f32[1,2,512]{2,1,0:T(2,128)} fusion(f32[1,2,512]{2,1,0:T(2,128)S(1)} %get-tuple-element.14, f32[1,2,512]{2,1,0:T(2,128)S(1)} %add.6, f32[1,2,512]{2,1,0:T(2,128)S(1)} %collective-permute-done.1), kind=kLoop, calls=%fused_computation | loop fusion | flops 3072 | bytes 16384 | tf_op jit(solution)/shard_map/sub | solution.py:406
  (1 shorter events, 0.0 us)
Async XLA Ops:
  1.3 53.5 %copy-start = (f32[1,2,512]{2,1,0:T(2,128)S(1)}, f32[1,2,512]{2,1,0:T(2,128)}, u32[]{:S(2)}) copy-start(f32[1,2,512]{2,1,0:T(2,128)} %image.1) | copy-start | bytes 12292
  47.0 3.6 %collective-permute-start = (f32[1,2,512]{2,1,0:T(2,128)S(1)}, f32[1,2,512]{2,1,0:T(2,128)S(1)}, u32[]{:S(2)}, u32[]{:S(2)}) collective-permute-start(f32[1,2,512]{2,1,0:T(2,128)S(1)} %backward.1), channel_id=1, source_target_pairs={{0,1},{1,0},{2,3},{3,2},{4,5},{5,4},{6,7},{7,6},{8,9},{9,8},{10,11... | collective-permute-start | bytes 12296 | tf_op jit(solution)/shard_map/ppermute | solution.py:391
  50.5 6.4 %collective-permute-start.1 = (f32[1,2,512]{2,1,0:T(2,128)S(1)}, f32[1,2,512]{2,1,0:T(2,128)S(1)}, u32[]{:S(2)}, u32[]{:S(2)}) collective-permute-start(f32[1,2,512]{2,1,0:T(2,128)S(1)} %add.6), channel_id=1, source_target_pairs={{0,2},{2,0},{1,3},{3,1},{4,6},{6,4},{5,7},{7,5},{8,10},{10,8},{9,1... | collective-permute-start | bytes 12296 | tf_op jit(solution)/shard_map/ppermute | solution.py:392

commit v10 on v9

--- a/solution.py
+++ b/solution.py
@@ -142,15 +142,14 @@
     row = lax.broadcasted_iota(jnp.int32, x.shape, 0) & 15
     lane = lane_iota(x.shape)
 
+    following = jnp.where(row == 15, 0.0, pltpu.roll(x, x.shape[0] - 1, 0))
+    previous = jnp.where(row == 0, 0.0, pltpu.roll(x, 1, 0))
+
     def ahead(t):
-        rolled = pltpu.roll(x, LANES - t, 1)
-        after = jnp.where(row == 15, 0.0, pltpu.roll(rolled, x.shape[0] - 1, 0))
-        return jnp.where(lane >= LANES - t, after, rolled)
+        return pltpu.roll(jnp.where(lane < t, following, x), LANES - t, 1)
 
     def behind(t):
-        rolled = pltpu.roll(x, t, 1)
-        before = jnp.where(row == 0, 0.0, pltpu.roll(rolled, 1, 0))
-        return jnp.where(lane < t, before, rolled)
+        return pltpu.roll(jnp.where(lane >= LANES - t, previous, x), t, 1)
 
     return ((behind(2) - ahead(2)) + 8.0 * (ahead(1) - behind(1))) * (1.0 / 12.0)
 

time: 57.7 us -> 57.7 us (level)
  no operation moved by 1% of the time
where the time goes in v10:
time: 57.7 us; the launch traced here: 57.5 us
  blocking collectives  37.8 us (66%)
  Pallas kernels  8.65 us (15%)
  starting transfers between devices  6.96 us (12%)
  waiting for transfers between devices  2.16 us (4%)
  between operations  1.31 us (2%)
  other arithmetic  0.6 us (1%)
    all_to_all x2, blocking collectives, on_device(): got = lax.all_to_all(sent, VOX, 0, 0, tiled=True)  37.8 us
    pallas_call x1, Pallas kernels, on_device(): pl.pallas_call(forward_kernel, out_shape=(jax.ShapeDtypeStruct((OWNERS, 2...  4.72 us
    ppermute x1, starting transfers between devices, on_device(): other = lax.ppermute(grad, 'z_hi', [(0, 1), (1, 0)])  4.22 us
    ppermute x1, starting transfers between devices, on_device(): grad = grad + lax.ppermute(grad, 'core', [(0, 1), (1, 0)])  2.74 us
    pallas_call x1, Pallas kernels, on_device(): pl.pallas_call(backward_kernel, out_shape=jax.ShapeDtypeStruct((1, 2, 512...  2.01 us
    ppermute x1, waiting for transfers between devices, on_device(): other = lax.ppermute(grad, 'z_hi', [(0, 1), (1, 0)])  1.33 us
  transfers between devices with their start and end apart: 2, of which 2 were waited for; matrix products, arithmetic and copies ran while one was open for 0% of the time, Pallas kernels for 1%

profile of v10, /device:TPU:1, one launch (start us, length us, event | category | flops | bytes accessed | tf_op | source)
XLA Modules:
  0.0 57.5 jit_solution(16999243852832312398)
XLA Ops:
  1.3 0.0 copy-start
  1.3 4.7 %forward.1 = (bf16[64,2,768]{2,1,0:T(2,128)(2,1)S(1)}, f32[64,128]{1,0:T(8,128)S(1)}, bf16[5,1024,1024]{2,1,0:T(8,128)(2,1)S(1)}, s32[8,128]{1,0:T(8,128)S(1)}) custom-call(s32[1,1,5]{2,1,0:T(1,128)} %ids_hbm.1, s32[1,1,5]{2,1,0:T(1,128)} %starts_hbm.1, s32[1,1]{1,0:T(1,128)S(6)} %copy.8.counts, f32[1,2,512]{2,1,0:T(2,128)} %image.1, ...), custom_call_target="tpu_custom_call" | custom-call | tf_op jit(solution)/shard_map/forward/pallas_call | solution.py:338
  6.0 22.4 %all_to_all.10.got = bf16[64,2,768]{2,1,0:T(2,128)(2,1)S(1)} all-to-all(bf16[64,2,768]{2,1,0:T(2,128)(2,1)S(1)} %get-tuple-element.10), channel_id=1, replica_groups=mesh['y'=4,'x'=4,'z_lo'=4,'z_hi'=2,'core'=2] {'y','x','z_lo'}, dimensions={0} | all-to-all | bytes 393216 | tf_op jit(solution)/shard_map/all_to_all | solution.py:367
  28.4 1.1 %owner.1 = (bf16[64,2,768]{2,1,0:T(2,128)(2,1)S(1)}, f32[64,128]{1,0:T(8,128)S(1)}) custom-call(bf16[64,2,768]{2,1,0:T(2,128)(2,1)S(1)} %all_to_all.10.got, f32[64,128]{1,0:T(8,128)S(1)} %get-tuple-element.11.spread), custom_call_target="tpu_custom_call" | custom-call | tf_op jit(solution)/shard_map/owner/pallas_call | solution.py:368
  29.6 15.4 %all_to_all.11.got = bf16[64,2,768]{2,1,0:T(2,128)(2,1)S(1)} all-to-all(bf16[64,2,768]{2,1,0:T(2,128)(2,1)S(1)} %get-tuple-element.12), channel_id=1, replica_groups=mesh['y'=4,'x'=4,'z_lo'=4,'z_hi'=2,'core'=2] {'y','x','z_lo'}, dimensions={0} | all-to-all | bytes 393216 | tf_op jit(solution)/shard_map/all_to_all | solution.py:380
  45.0 2.0 %backward.1 = f32[1,2,512]{2,1,0:T(2,128)S(1)} custom-call(s32[8,128]{1,0:T(8,128)S(1)} %get-tuple-element.15.table, bf16[64,2,768]{2,1,0:T(2,128)(2,1)S(1)} %all_to_all.11.got, bf16[5,1024,1024]{2,1,0:T(8,128)(2,1)S(1)} %get-tuple-element.16.held), custom_call_target="tpu_custom_call" | custom-call | tf_op jit(solution)/shard_map/backward/pallas_call | solution.py:381
  47.0 2.7 %collective-permute-start = (f32[1,2,512]{2,1,0:T(2,128)S(1)}, f32[1,2,512]{2,1,0:T(2,128)S(1)}, u32[]{:S(2)}, u32[]{:S(2)}) collective-permute-start(f32[1,2,512]{2,1,0:T(2,128)S(1)} %backward.1), channel_id=1, source_target_pairs={{0,1},{1,0},{2,3},{3,2},{4,5},{5,4},{6,7},{7,6},{8,9},{9,8},{10,11... | collective-permute-start | bytes 12296 | tf_op jit(solution)/shard_map/ppermute | solution.py:390
  49.7 0.8 %collective-permute-done = f32[1,2,512]{2,1,0:T(2,128)S(1)} collective-permute-done((f32[1,2,512]{2,1,0:T(2,128)S(1)}, f32[1,2,512]{2,1,0:T(2,128)S(1)}, u32[]{:S(2)}, u32[]{:S(2)}) %collective-permute-start) | collective-permute-done | bytes 4128 | tf_op jit(solution)/shard_map/ppermute | solution.py:390
  50.5 4.2 %collective-permute-start.1 = (f32[1,2,512]{2,1,0:T(2,128)S(1)}, f32[1,2,512]{2,1,0:T(2,128)S(1)}, u32[]{:S(2)}, u32[]{:S(2)}) collective-permute-start(f32[1,2,512]{2,1,0:T(2,128)S(1)} %add.6), channel_id=1, source_target_pairs={{0,2},{2,0},{1,3},{3,1},{4,6},{6,4},{5,7},{7,5},{8,10},{10,8},{9,1... | collective-permute-start | bytes 12296 | tf_op jit(solution)/shard_map/ppermute | solution.py:391
  54.8 0.0 copy-done
  54.8 0.8 %smooth.1 = (f32[1,2,512]{2,1,0:T(2,128)S(1)}, f32[1,4,2048]{2,1,0:T(4,128)}) custom-call(bf16[64,2,768]{2,1,0:T(2,128)(2,1)S(1)} %all_to_all.11.got, f32[1,2,512]{2,1,0:T(2,128)S(1)} %copy-done, f32[64,128]{1,0:T(8,128)S(1)} %get-tuple-element.13.resid), custom_call_target="tpu_custom_call" | custom-call | flops 100000 | bytes 524288 | tf_op jit(solution)/shard_map/smooth/pallas_call | solution.py:392
  55.6 1.3 %collective-permute-done.1 = f32[1,2,512]{2,1,0:T(2,128)S(1)} collective-permute-done((f32[1,2,512]{2,1,0:T(2,128)S(1)}, f32[1,2,512]{2,1,0:T(2,128)S(1)}, u32[]{:S(2)}, u32[]{:S(2)}) %collective-permute-start.1) | collective-permute-done | bytes 4128 | tf_op jit(solution)/shard_map/ppermute | solution.py:391
  56.9 0.6 %multiply_subtract_fusion = f32[1,2,512]{2,1,0:T(2,128)} fusion(f32[1,2,512]{2,1,0:T(2,128)S(1)} %get-tuple-element.14, f32[1,2,512]{2,1,0:T(2,128)S(1)} %add.6, f32[1,2,512]{2,1,0:T(2,128)S(1)} %collective-permute-done.1), kind=kLoop, calls=%fused_computation | loop fusion | flops 3072 | bytes 16384 | tf_op jit(solution)/shard_map/sub | solution.py:405
  (1 shorter events, 0.0 us)
Async XLA Ops:
  1.3 53.5 %copy-start = (f32[1,2,512]{2,1,0:T(2,128)S(1)}, f32[1,2,512]{2,1,0:T(2,128)}, u32[]{:S(2)}) copy-start(f32[1,2,512]{2,1,0:T(2,128)} %image.1) | copy-start | bytes 12292
  47.0 3.6 %collective-permute-start = (f32[1,2,512]{2,1,0:T(2,128)S(1)}, f32[1,2,512]{2,1,0:T(2,128)S(1)}, u32[]{:S(2)}, u32[]{:S(2)}) collective-permute-start(f32[1,2,512]{2,1,0:T(2,128)S(1)} %backward.1), channel_id=1, source_target_pairs={{0,1},{1,0},{2,3},{3,2},{4,5},{5,4},{6,7},{7,6},{8,9},{9,8},{10,11... | collective-permute-start | bytes 12296 | tf_op jit(solution)/shard_map/ppermute | solution.py:390
  50.5 6.4 %collective-permute-start.1 = (f32[1,2,512]{2,1,0:T(2,128)S(1)}, f32[1,2,512]{2,1,0:T(2,128)S(1)}, u32[]{:S(2)}, u32[]{:S(2)}) collective-permute-start(f32[1,2,512]{2,1,0:T(2,128)S(1)} %add.6), channel_id=1, source_target_pairs={{0,2},{2,0},{1,3},{3,1},{4,6},{6,4},{5,7},{7,5},{8,10},{10,8},{9,1... | collective-permute-start | bytes 12296 | tf_op jit(solution)/shard_map/ppermute | solution.py:391

commit v11 on v9

--- a/solution.py
+++ b/solution.py
@@ -18,7 +18,7 @@
 WIDTH = TILES * LANES
 OWNERS = 64
 ON_MATRIX = 2
-AHEAD = 2
+AHEAD = 1
 PLACE = 2048
 LIVE = 16 * PLACE
 STEP_SIZE = 0.25

time: 57.7 us -> 57.7 us (level)
  no operation moved by 1% of the time
where the time goes in v11:
time: 57.7 us; the launch traced here: 57.5 us
  blocking collectives  37.8 us (66%)
  Pallas kernels  8.64 us (15%)
  starting transfers between devices  6.94 us (12%)
  waiting for transfers between devices  2.16 us (4%)
  between operations  1.31 us (2%)
  other arithmetic  0.6 us (1%)
    all_to_all x2, blocking collectives, on_device(): got = lax.all_to_all(sent, VOX, 0, 0, tiled=True)  37.8 us
    pallas_call x1, Pallas kernels, on_device(): pl.pallas_call(forward_kernel, out_shape=(jax.ShapeDtypeStruct((OWNERS, 2...  4.72 us
    ppermute x1, starting transfers between devices, on_device(): other = lax.ppermute(grad, 'z_hi', [(0, 1), (1, 0)])  4.21 us
    ppermute x1, starting transfers between devices, on_device(): grad = grad + lax.ppermute(grad, 'core', [(0, 1), (1, 0)])  2.73 us
    pallas_call x1, Pallas kernels, on_device(): pl.pallas_call(backward_kernel, out_shape=jax.ShapeDtypeStruct((1, 2, 512...  2.01 us
    ppermute x1, waiting for transfers between devices, on_device(): other = lax.ppermute(grad, 'z_hi', [(0, 1), (1, 0)])  1.34 us
  transfers between devices with their start and end apart: 2, of which 2 were waited for; matrix products, arithmetic and copies ran while one was open for 0% of the time, Pallas kernels for 1%

profile of v11, /device:TPU:1, one launch (start us, length us, event | category | flops | bytes accessed | tf_op | source)
XLA Modules:
  0.0 57.5 jit_solution(18257090178848297715)
XLA Ops:
  1.3 0.0 copy-start
  1.3 4.7 %forward.1 = (bf16[64,2,768]{2,1,0:T(2,128)(2,1)S(1)}, f32[64,128]{1,0:T(8,128)S(1)}, bf16[5,1024,1024]{2,1,0:T(8,128)(2,1)S(1)}, s32[8,128]{1,0:T(8,128)S(1)}) custom-call(s32[1,1,5]{2,1,0:T(1,128)} %ids_hbm.1, s32[1,1,5]{2,1,0:T(1,128)} %starts_hbm.1, s32[1,1]{1,0:T(1,128)S(6)} %copy.8.counts, f32[1,2,512]{2,1,0:T(2,128)} %image.1, ...), custom_call_target="tpu_custom_call" | custom-call | tf_op jit(solution)/shard_map/forward/pallas_call | solution.py:339
  6.0 22.4 %all_to_all.10.got = bf16[64,2,768]{2,1,0:T(2,128)(2,1)S(1)} all-to-all(bf16[64,2,768]{2,1,0:T(2,128)(2,1)S(1)} %get-tuple-element.10), channel_id=1, replica_groups=mesh['y'=4,'x'=4,'z_lo'=4,'z_hi'=2,'core'=2] {'y','x','z_lo'}, dimensions={0} | all-to-all | bytes 393216 | tf_op jit(solution)/shard_map/all_to_all | solution.py:368
  28.4 1.1 %owner.1 = (bf16[64,2,768]{2,1,0:T(2,128)(2,1)S(1)}, f32[64,128]{1,0:T(8,128)S(1)}) custom-call(bf16[64,2,768]{2,1,0:T(2,128)(2,1)S(1)} %all_to_all.10.got, f32[64,128]{1,0:T(8,128)S(1)} %get-tuple-element.11.spread), custom_call_target="tpu_custom_call" | custom-call | tf_op jit(solution)/shard_map/owner/pallas_call | solution.py:369
  29.5 15.4 %all_to_all.11.got = bf16[64,2,768]{2,1,0:T(2,128)(2,1)S(1)} all-to-all(bf16[64,2,768]{2,1,0:T(2,128)(2,1)S(1)} %get-tuple-element.12), channel_id=1, replica_groups=mesh['y'=4,'x'=4,'z_lo'=4,'z_hi'=2,'core'=2] {'y','x','z_lo'}, dimensions={0} | all-to-all | bytes 393216 | tf_op jit(solution)/shard_map/all_to_all | solution.py:381
  45.0 2.0 %backward.1 = f32[1,2,512]{2,1,0:T(2,128)S(1)} custom-call(s32[8,128]{1,0:T(8,128)S(1)} %get-tuple-element.15.table, bf16[64,2,768]{2,1,0:T(2,128)(2,1)S(1)} %all_to_all.11.got, bf16[5,1024,1024]{2,1,0:T(8,128)(2,1)S(1)} %get-tuple-element.16.held), custom_call_target="tpu_custom_call" | custom-call | tf_op jit(solution)/shard_map/backward/pallas_call | solution.py:382
  47.0 2.7 %collective-permute-start = (f32[1,2,512]{2,1,0:T(2,128)S(1)}, f32[1,2,512]{2,1,0:T(2,128)S(1)}, u32[]{:S(2)}, u32[]{:S(2)}) collective-permute-start(f32[1,2,512]{2,1,0:T(2,128)S(1)} %backward.1), channel_id=1, source_target_pairs={{0,1},{1,0},{2,3},{3,2},{4,5},{5,4},{6,7},{7,6},{8,9},{9,8},{10,11... | collective-permute-start | bytes 12296 | tf_op jit(solution)/shard_map/ppermute | solution.py:391
  49.7 0.8 %collective-permute-done = f32[1,2,512]{2,1,0:T(2,128)S(1)} collective-permute-done((f32[1,2,512]{2,1,0:T(2,128)S(1)}, f32[1,2,512]{2,1,0:T(2,128)S(1)}, u32[]{:S(2)}, u32[]{:S(2)}) %collective-permute-start) | collective-permute-done | bytes 4128 | tf_op jit(solution)/shard_map/ppermute | solution.py:391
  50.5 4.2 %collective-permute-start.1 = (f32[1,2,512]{2,1,0:T(2,128)S(1)}, f32[1,2,512]{2,1,0:T(2,128)S(1)}, u32[]{:S(2)}, u32[]{:S(2)}) collective-permute-start(f32[1,2,512]{2,1,0:T(2,128)S(1)} %add.6), channel_id=1, source_target_pairs={{0,2},{2,0},{1,3},{3,1},{4,6},{6,4},{5,7},{7,5},{8,10},{10,8},{9,1... | collective-permute-start | bytes 12296 | tf_op jit(solution)/shard_map/ppermute | solution.py:392
  54.7 0.0 copy-done
  54.8 0.8 %smooth.1 = (f32[1,2,512]{2,1,0:T(2,128)S(1)}, f32[1,4,2048]{2,1,0:T(4,128)}) custom-call(bf16[64,2,768]{2,1,0:T(2,128)(2,1)S(1)} %all_to_all.11.got, f32[1,2,512]{2,1,0:T(2,128)S(1)} %copy-done, f32[64,128]{1,0:T(8,128)S(1)} %get-tuple-element.13.resid), custom_call_target="tpu_custom_call" | custom-call | flops 100000 | bytes 524288 | tf_op jit(solution)/shard_map/smooth/pallas_call | solution.py:393
  55.6 1.3 %collective-permute-done.1 = f32[1,2,512]{2,1,0:T(2,128)S(1)} collective-permute-done((f32[1,2,512]{2,1,0:T(2,128)S(1)}, f32[1,2,512]{2,1,0:T(2,128)S(1)}, u32[]{:S(2)}, u32[]{:S(2)}) %collective-permute-start.1) | collective-permute-done | bytes 4128 | tf_op jit(solution)/shard_map/ppermute | solution.py:392
  56.9 0.6 %multiply_subtract_fusion = f32[1,2,512]{2,1,0:T(2,128)} fusion(f32[1,2,512]{2,1,0:T(2,128)S(1)} %get-tuple-element.14, f32[1,2,512]{2,1,0:T(2,128)S(1)} %add.6, f32[1,2,512]{2,1,0:T(2,128)S(1)} %collective-permute-done.1), kind=kLoop, calls=%fused_computation | loop fusion | flops 3072 | bytes 16384 | tf_op jit(solution)/shard_map/sub | solution.py:406
  (1 shorter events, 0.0 us)
Async XLA Ops:
  1.3 53.5 %copy-start = (f32[1,2,512]{2,1,0:T(2,128)S(1)}, f32[1,2,512]{2,1,0:T(2,128)}, u32[]{:S(2)}) copy-start(f32[1,2,512]{2,1,0:T(2,128)} %image.1) | copy-start | bytes 12292
  47.0 3.6 %collective-permute-start = (f32[1,2,512]{2,1,0:T(2,128)S(1)}, f32[1,2,512]{2,1,0:T(2,128)S(1)}, u32[]{:S(2)}, u32[]{:S(2)}) collective-permute-start(f32[1,2,512]{2,1,0:T(2,128)S(1)} %backward.1), channel_id=1, source_target_pairs={{0,1},{1,0},{2,3},{3,2},{4,5},{5,4},{6,7},{7,6},{8,9},{9,8},{10,11... | collective-permute-start | bytes 12296 | tf_op jit(solution)/shard_map/ppermute | solution.py:391
  50.5 6.4 %collective-permute-start.1 = (f32[1,2,512]{2,1,0:T(2,128)S(1)}, f32[1,2,512]{2,1,0:T(2,128)S(1)}, u32[]{:S(2)}, u32[]{:S(2)}) collective-permute-start(f32[1,2,512]{2,1,0:T(2,128)S(1)} %add.6), channel_id=1, source_target_pairs={{0,2},{2,0},{1,3},{3,1},{4,6},{6,4},{5,7},{7,5},{8,10},{10,8},{9,1... | collective-permute-start | bytes 12296 | tf_op jit(solution)/shard_map/ppermute | solution.py:392
